TPU v7x, 256 devices: a whole 4x4x8 slice. The times are simulated.
256 devices in a mesh: section: 4 (over x), expert: 64 (over z, y, core).
Axes of the slice: x: 4, y: 4, z: 8, core: 2. Of those that a mesh axis runs over, the one named last changes fastest.
Arguments:
- inputs: bfloat16 [2, 4096, 2048], P(None, 'expert'), may hold values from -45 to 45
- cotangent: bfloat16 [2, 4096, 2048], P(None, 'expert'), may hold values from -6 to 6
- lengths: int32 [2, 64], P(None, 'expert'), may hold values from 32 to 64, as said below
- norm_gain: float32 [4, 2048], P('section'), may hold values from 0.1 to 1.9
- router: bfloat16 [4, 2048, 64], P('section'), may hold values from -0.125 to 0.125
- expert_in: bfloat16 [4, 64, 2048, 1536], P('section', 'expert'), may hold values from -0.125 to 0.125
- expert_out: bfloat16 [4, 64, 768, 2048], P('section', 'expert'), may hold values from -0.21875 to 0.21875
- routes: int32 [4, 2, 4096, 2], P('section', None, 'expert'), may hold values from 0 to 63, as said below
Outputs:
- section_grads: bfloat16 [4, 2, 4096, 2048], P('section', None, 'expert')
- router_grad: float32 [4, 2048, 64], P('section')
- gain_grad: float32 [4, 2048], P('section')
Inputs may be any that keep to these rules, and one draw needn't show every extreme that they name: `lengths`: sequence b of a micro-batch fills positions b * 64 to b * 64 + length - 1; the rest is padding. Each micro-batch has a sequence of length 64. `routes`: each row names 2 different experts. Among the rows of one sequence for one section and micro-batch no expert is named more than 2 times; for each section and micro-batch one expert is named exactly 2 times within the first 32 rows of every sequence. For each section and micro-batch the experts fall into two halves, a row's first choice in one and its second in the other.
All inputs are finite; a program needn't handle non-finite values.
Results may differ from a plain program's by a relative error of at most 0.024.
Values may be sent and summed in bfloat16 or wider, within the bound.
A program may use at most 128 MiB of HBM per device.

v0:
```python
import jax
import jax.numpy as jnp
from jax import lax
from jax.sharding import PartitionSpec as P

EPSILON = 1e-06


def shifted(block, axis, distance):
    devices = range(lax.axis_size(axis))
    route = [(i - distance, i) for i in devices if i - distance in devices]
    return lax.ppermute(block, axis, route)


def normalize(hidden_in, gain_row):
    values = hidden_in.astype(jnp.float32)
    scale_inv = lax.rsqrt(jnp.mean(values * values, axis=-1, keepdims=True) + EPSILON)
    normed = (values * scale_inv * gain_row).astype(jnp.bfloat16)
    return (values, scale_inv, normed)


def expert_mix(row_block, weight_in):
    return jnp.dot(row_block, weight_in, preferred_element_type=jnp.float32)


def expert_apply(row_block, weight_in, weight_out):
    hidden = weight_out.shape[0]
    mixed_rows = expert_mix(row_block, weight_in)
    gate_part = mixed_rows[:, :hidden]
    up_part = mixed_rows[:, hidden:]
    activated = (gate_part * jax.nn.sigmoid(gate_part) * up_part).astype(jnp.bfloat16)
    result = jnp.dot(activated, weight_out, preferred_element_type=jnp.float32).astype(jnp.bfloat16)
    return (result, mixed_rows)


def expert_adjoint(mixed_rows, grad_rows, weight_in, weight_out):
    hidden = weight_out.shape[0]
    gate_part = mixed_rows[:, :hidden]
    up_part = mixed_rows[:, hidden:]
    act_grad = lax.dot_general(
        grad_rows, weight_out, (((1,), (1,)), ((), ())), preferred_element_type=jnp.float32
    )
    sigmoid_gate = jax.nn.sigmoid(gate_part)
    gate_grad = act_grad * up_part * sigmoid_gate * (1.0 + gate_part * (1.0 - sigmoid_gate))
    up_grad = act_grad * gate_part * sigmoid_gate
    joined = jnp.concatenate([gate_grad, up_grad], axis=1).astype(jnp.bfloat16)
    return lax.dot_general(
        joined, weight_in, (((1,), (1,)), ((), ())), preferred_element_type=jnp.float32
    ).astype(jnp.bfloat16)


def choice_weights(normed, router_local, route_rows):
    experts = router_local.shape[1]
    logits = jnp.dot(normed, router_local, preferred_element_type=jnp.float32)
    expert_codes = lax.broadcasted_iota(jnp.int32, (1, 1, experts), 2)
    chosen = route_rows[:, :, None] == expert_codes
    picked = jnp.sum(jnp.where(chosen, logits[:, None, :], 0.0), axis=-1)
    weights = jax.nn.sigmoid(picked - picked[:, ::-1])
    return (chosen, weights)


def slot_tables(chosen, live_rows, capacity):
    tokens_here, choice_count, experts = chosen.shape
    marked = (
        (chosen & live_rows[:, None, None])
        .reshape(tokens_here * choice_count, experts)
        .astype(jnp.int32)
    )
    earlier = jnp.cumsum(marked, axis=0) - marked
    position = jnp.sum(earlier * marked, axis=1)
    expert_codes = lax.broadcasted_iota(jnp.int32, (1, experts), 1)
    target = jnp.sum(marked * expert_codes, axis=1)
    present = jnp.sum(marked, axis=1) > 0
    slot_of = jnp.where(present, target * capacity + position, -1).reshape(
        tokens_here, choice_count
    )
    slot_codes = lax.broadcasted_iota(jnp.int32, (choice_count, experts * capacity, tokens_here), 1)
    return (jnp.transpose(slot_of)[:, None, :] == slot_codes).astype(jnp.bfloat16)


def store_at(buffer, new_value, slot_index, keep_flag):
    previous = lax.dynamic_index_in_dim(buffer, slot_index, 0, keepdims=False)
    return lax.dynamic_update_index_in_dim(
        buffer, jnp.where(keep_flag, new_value, previous), slot_index, 0
    )


def local(inputs, cotangent, lengths, norm_gain, router, expert_in, expert_out, routes):
    micro_count, tokens_here, model_width = inputs.shape
    sections = lax.axis_size("section")
    section_id = lax.axis_index("section")
    router_local = router[0]
    experts = router_local.shape[1]
    choice_count = routes.shape[3]
    capacity = choice_count * tokens_here // experts
    gain_row = norm_gain[0]
    weight_in = expert_in[0, 0]
    weight_out = expert_out[0, 0]
    hidden = weight_out.shape[0]
    positions = lax.broadcasted_iota(jnp.int32, (micro_count, tokens_here), 1)
    live_all = positions < lengths
    route_all = routes[0]
    ticks = sections + micro_count - 1
    inbox_rows = jnp.zeros((tokens_here, model_width), jnp.bfloat16)
    stored_inputs = jnp.zeros((micro_count, tokens_here, model_width), jnp.bfloat16)
    stored_outputs = jnp.zeros((micro_count, choice_count, tokens_here, model_width), jnp.float32)
    stored_mixed = jnp.zeros((micro_count, experts, capacity, 2 * hidden), jnp.float32)
    for tick_index in range(ticks):
        micro_index = tick_index - section_id
        inside = (micro_index >= 0) & (micro_index < micro_count)
        working = inside
        clipped = jnp.clip(micro_index, 0, micro_count - 1)
        arriving = lax.dynamic_index_in_dim(inputs, clipped, 0, keepdims=False)
        hidden_in = jnp.where(section_id == 0, arriving, inbox_rows)
        values, scale_inv, normed = normalize(hidden_in, gain_row)
        route_rows = lax.dynamic_index_in_dim(route_all, clipped, 0, keepdims=False)
        live_rows = lax.dynamic_index_in_dim(live_all, clipped, 0, keepdims=False)
        chosen, weights = choice_weights(normed, router_local, route_rows)
        pair_table = slot_tables(chosen, live_rows, capacity)
        slot_table = jnp.sum(pair_table, axis=0)
        outgoing = jnp.dot(slot_table, normed, preferred_element_type=jnp.float32).astype(
            jnp.bfloat16
        )
        outgoing = outgoing.reshape(experts, capacity, model_width)
        run_received = lax.all_to_all(outgoing, "expert", split_axis=0, concat_axis=0, tiled=True)
        row_shape = run_received.shape

        def compute(row_block):
            return expert_apply(row_block, weight_in, weight_out)

        def skip_work(row_block):
            return (
                jnp.zeros(row_block.shape, jnp.bfloat16),
                jnp.zeros((row_block.shape[0], 2 * hidden), jnp.float32),
            )

        run_result, mixed_rows = lax.cond(
            working, compute, skip_work, run_received.reshape(-1, model_width)
        )
        returned = lax.all_to_all(
            run_result.reshape(row_shape), "expert", split_axis=0, concat_axis=0, tiled=True
        )
        returned, mixed_rows = (
            returned,
            mixed_rows.reshape(row_shape[0], row_shape[1], 2 * hidden),
        )
        expert_rows = returned.reshape(experts * capacity, model_width)
        per_choice = jnp.einsum(
            "kst,sd->ktd", pair_table, expert_rows, preferred_element_type=jnp.float32
        )
        combined = jnp.sum(jnp.transpose(weights)[:, :, None] * per_choice, axis=0)
        leaving = (values + combined).astype(jnp.bfloat16)
        stored_inputs = store_at(stored_inputs, hidden_in, clipped, inside)
        stored_outputs = store_at(stored_outputs, per_choice, clipped, inside)
        stored_mixed = store_at(stored_mixed, mixed_rows, clipped, inside)
        inbox_rows = shifted(leaving, "section", 1)
    inbox_rows = jnp.zeros((tokens_here, model_width), jnp.bfloat16)
    router_total = jnp.zeros((model_width, experts), jnp.float32)
    gain_total = jnp.zeros((model_width,), jnp.float32)
    grads_out = jnp.zeros((micro_count, tokens_here, model_width), jnp.bfloat16)
    for tick_index in range(ticks):
        micro_index = tick_index - (sections - 1 - section_id)
        inside = (micro_index >= 0) & (micro_index < micro_count)
        working = inside
        clipped = jnp.clip(micro_index, 0, micro_count - 1)
        arriving = lax.dynamic_index_in_dim(cotangent, clipped, 0, keepdims=False)
        grad_in = jnp.where(section_id == sections - 1, arriving, inbox_rows)
        grad_values = grad_in.astype(jnp.float32)
        hidden_in = lax.dynamic_index_in_dim(stored_inputs, clipped, 0, keepdims=False)
        values, scale_inv, normed = normalize(hidden_in, gain_row)
        route_rows = lax.dynamic_index_in_dim(route_all, clipped, 0, keepdims=False)
        live_rows = lax.dynamic_index_in_dim(live_all, clipped, 0, keepdims=False)
        chosen, weights = choice_weights(normed, router_local, route_rows)
        pair_table = slot_tables(chosen, live_rows, capacity)
        per_choice = lax.dynamic_index_in_dim(stored_outputs, clipped, 0, keepdims=False)
        choice_grad = jnp.sum(grad_values[None] * per_choice, axis=-1)
        first_grad = weights[:, 0] * weights[:, 1] * (choice_grad[0] - choice_grad[1])
        pick_grad = jnp.stack([first_grad, -first_grad], axis=1)
        logit_grad = jnp.sum(jnp.where(chosen, pick_grad[:, :, None], 0.0), axis=1).astype(
            jnp.bfloat16
        )
        output_grad = (jnp.transpose(weights)[:, :, None] * grad_values[None]).astype(jnp.bfloat16)
        grad_send = jnp.einsum(
            "kst,ktd->sd", pair_table, output_grad, preferred_element_type=jnp.float32
        )
        grad_send = grad_send.astype(jnp.bfloat16).reshape(experts, capacity, model_width)
        received = lax.all_to_all(grad_send, "expert", split_axis=0, concat_axis=0, tiled=True)
        mixed_flat = lax.dynamic_index_in_dim(stored_mixed, clipped, 0, keepdims=False).reshape(
            -1, 2 * hidden
        )

        def compute_kept(packed):
            return expert_adjoint(packed[0], packed[1], weight_in, weight_out)

        def skip_kept(packed):
            return jnp.zeros(packed[1].shape, jnp.bfloat16)

        result = lax.cond(
            working, compute_kept, skip_kept, (mixed_flat, received.reshape(-1, model_width))
        )
        returned = lax.all_to_all(
            result.reshape(received.shape), "expert", split_axis=0, concat_axis=0, tiled=True
        )
        rows_back = returned.reshape(experts * capacity, model_width)
        normed_grad = jnp.sum(
            jnp.einsum("kst,sd->ktd", pair_table, rows_back, preferred_element_type=jnp.float32),
            axis=0,
        )
        normed_grad = normed_grad + lax.dot_general(
            logit_grad, router_local, (((1,), (1,)), ((), ())), preferred_element_type=jnp.float32
        )
        centred = values * scale_inv
        scaled_grad = normed_grad * gain_row
        input_grad = grad_values + scale_inv * (
            scaled_grad - centred * jnp.mean(scaled_grad * centred, axis=-1, keepdims=True)
        )
        leaving = input_grad.astype(jnp.bfloat16)
        router_piece = lax.dot_general(
            normed, logit_grad, (((0,), (0,)), ((), ())), preferred_element_type=jnp.float32
        )
        router_total = router_total + jnp.where(working, router_piece, 0.0)
        gain_total = gain_total + jnp.where(working, jnp.sum(normed_grad * centred, axis=0), 0.0)
        grads_out = store_at(grads_out, leaving, clipped, inside)
        inbox_rows = shifted(leaving, "section", -1)
    router_sum, gain_sum = lax.psum((router_total, gain_total), "expert")
    denominator = micro_count * choice_count * tokens_here
    return (grads_out[None], (router_sum / denominator)[None], (gain_sum / denominator)[None])


def solution(mesh):
    in_specs = (
        P(None, "expert", None),
        P(None, "expert", None),
        P(None, "expert"),
        P("section", None),
        P("section", None, None),
        P("section", "expert", None, None),
        P("section", "expert", None, None),
        P("section", None, "expert", None),
    )
    out_specs = (P("section", None, "expert", None), P("section", None, None), P("section", None))
    return jax.shard_map(local, mesh=mesh, in_specs=in_specs, out_specs=out_specs, check_vma=False)
```

profile of v0, /device:TPU:1, one launch (start us, length us, event | category | flops | bytes accessed | tf_op | source)
XLA Modules:
  0.0 1068.1 jit_solution(18199938061833508150)
XLA Ops:
  15.9 13.1 %all-to-all-start = ((bf16[64,2,2048]{2,1,0:T(2,128)(2,1)}), bf16[64,2,2048]{2,1,0:T(2,128)(2,1)S(1)}, u32[]{:S(2)}, u32[]{:S(2)}) async-start(bf16[64,2,2048]{2,1,0:T(2,128)(2,1)} %reshape.765), calls=%async_computation | async-start | bytes 1048576 | tf_op jit(solution)/shard_map/all_to_all | solution.py:125
  30.3 16.5 %all-to-all-done = bf16[64,2,2048]{2,1,0:T(2,128)(2,1)S(1)} async-done(((bf16[64,2,2048]{2,1,0:T(2,128)(2,1)}), bf16[64,2,2048]{2,1,0:T(2,128)(2,1)S(1)}, u32[]{:S(2)}, u32[]{:S(2)}) %all-to-all-start) | async-done | bytes 524320 | tf_op jit(solution)/shard_map/all_to_all | solution.py:125
  46.7 6.9 conditional.10
  46.9 3.8 fusion.376
  54.8 5.7 all-to-all-start.1
  62.6 15.6 %all-to-all-done.1 = bf16[64,2,2048]{2,1,0:T(2,128)(2,1)S(1)} async-done(((bf16[64,2,2048]{2,1,0:T(2,128)(2,1)}), bf16[64,2,2048]{2,1,0:T(2,128)(2,1)S(1)}, u32[]{:S(2)}, u32[]{:S(2)}) %all-to-all-start.1) | async-done | bytes 524320 | tf_op jit(solution)/shard_map/all_to_all | solution.py:140
  81.8 4.9 collective-permute-done
  88.4 6.5 all-to-all-start.2
  97.8 14.6 %all-to-all-done.2 = bf16[64,2,2048]{2,1,0:T(2,128)(2,1)S(1)} async-done(((bf16[64,2,2048]{2,1,0:T(2,128)(2,1)}), bf16[64,2,2048]{2,1,0:T(2,128)(2,1)S(1)}, u32[]{:S(2)}, u32[]{:S(2)}) %all-to-all-start.2) | async-done | bytes 524320 | tf_op jit(solution)/shard_map/all_to_all | solution.py:125
  112.4 7.7 conditional.11
  112.6 3.8 fusion.377
  116.9 3.3 convolution_convert_fusion.1
  122.6 5.7 all-to-all-start.3
  129.2 16.9 %all-to-all-done.3 = bf16[64,2,2048]{2,1,0:T(2,128)(2,1)S(1)} async-done(((bf16[64,2,2048]{2,1,0:T(2,128)(2,1)}), bf16[64,2,2048]{2,1,0:T(2,128)(2,1)S(1)}, u32[]{:S(2)}, u32[]{:S(2)}) %all-to-all-start.3) | async-done | bytes 524320 | tf_op jit(solution)/shard_map/all_to_all | solution.py:140
  147.7 4.3 collective-permute-start.1
  152.9 4.3 collective-permute-done.1
  158.9 6.2 all-to-all-start.4
  169.5 13.2 %all-to-all-done.4 = bf16[64,2,2048]{2,1,0:T(2,128)(2,1)S(1)} async-done(((bf16[64,2,2048]{2,1,0:T(2,128)(2,1)}), bf16[64,2,2048]{2,1,0:T(2,128)(2,1)S(1)}, u32[]{:S(2)}, u32[]{:S(2)}) %all-to-all-start.4) | async-done | bytes 524320 | tf_op jit(solution)/shard_map/all_to_all | solution.py:125
  184.2 6.0 all-to-all-start.5
  193.4 14.4 %all-to-all-done.5 = bf16[64,2,2048]{2,1,0:T(2,128)(2,1)} async-done(((bf16[64,2,2048]{2,1,0:T(2,128)(2,1)}), bf16[64,2,2048]{2,1,0:T(2,128)(2,1)}, u32[]{:S(2)}, u32[]{:S(2)}) %all-to-all-start.5) | async-done | bytes 524320 | tf_op jit(solution)/shard_map/all_to_all | solution.py:140
  213.3 10.8 %collective-permute-start.2 = (bf16[64,2048]{1,0:T(8,128)(2,1)S(1)}, bf16[64,2048]{1,0:T(8,128)(2,1)S(1)}, u32[]{:S(2)}, u32[]{:S(2)}) collective-permute-start(bf16[64,2048]{1,0:T(8,128)(2,1)S(1)} %fusion.170), channel_id=1, source_target_pairs={{0,64},{64,128},{128,192},{1,65},{65,129},{129,193},{2,66},{66,130... | collective-permute-start | bytes 786440 | tf_op jit(solution)/shard_map/ppermute | solution.py:12
  225.0 4.4 collective-permute-done.2
  233.6 6.4 all-to-all-start.6
  240.0 2.7 select_dynamic-update-slice_fusion.3
  245.4 12.1 %all-to-all-done.6 = bf16[64,2,2048]{2,1,0:T(2,128)(2,1)} async-done(((bf16[64,2,2048]{2,1,0:T(2,128)(2,1)}), bf16[64,2,2048]{2,1,0:T(2,128)(2,1)}, u32[]{:S(2)}, u32[]{:S(2)}) %all-to-all-start.6) | async-done | bytes 524320 | tf_op jit(solution)/shard_map/all_to_all | solution.py:125
  261.7 5.9 all-to-all-start.7
  270.8 14.4 %all-to-all-done.7 = bf16[64,2,2048]{2,1,0:T(2,128)(2,1)} async-done(((bf16[64,2,2048]{2,1,0:T(2,128)(2,1)}), bf16[64,2,2048]{2,1,0:T(2,128)(2,1)}, u32[]{:S(2)}, u32[]{:S(2)}) %all-to-all-start.7) | async-done | bytes 524320 | tf_op jit(solution)/shard_map/all_to_all | solution.py:140
  290.7 4.1 collective-permute-start.3
  295.7 4.4 collective-permute-done.3
  302.5 6.2 all-to-all-start.9
  314.8 11.6 %all-to-all-done.9 = bf16[64,2,2048]{2,1,0:T(2,128)(2,1)S(1)} async-done(((bf16[64,2,2048]{2,1,0:T(2,128)(2,1)}), bf16[64,2,2048]{2,1,0:T(2,128)(2,1)S(1)}, u32[]{:S(2)}, u32[]{:S(2)}) %all-to-all-start.9) | async-done | bytes 524320 | tf_op jit(solution)/shard_map/all_to_all | solution.py:125
  326.4 6.1 all-to-all-start.8
  341.5 8.6 all-to-all-done.8
  350.1 5.7 all-to-all-start.11
  365.1 8.4 all-to-all-done.11
  373.5 6.5 all-to-all-start.10
  385.2 12.2 %all-to-all-done.10 = bf16[64,2,2048]{2,1,0:T(2,128)(2,1)} async-done(((bf16[64,2,2048]{2,1,0:T(2,128)(2,1)}), bf16[64,2,2048]{2,1,0:T(2,128)(2,1)}, u32[]{:S(2)}, u32[]{:S(2)}) %all-to-all-start.10) | async-done | bytes 524320 | tf_op jit(solution)/shard_map/all_to_all | solution.py:201
  405.5 17.7 %collective-permute-done.4 = bf16[64,2048]{1,0:T(8,128)(2,1)} collective-permute-done((bf16[64,2048]{1,0:T(8,128)(2,1)}, bf16[64,2048]{1,0:T(8,128)(2,1)}, u32[]{:S(2)}, u32[]{:S(2)}) %collective-permute-start.4) | collective-permute-done | bytes 262176 | tf_op jit(solution)/shard_map/ppermute | solution.py:12
  427.7 6.1 all-to-all-start.12
  437.3 14.1 %all-to-all-done.12 = bf16[64,2,2048]{2,1,0:T(2,128)(2,1)} async-done(((bf16[64,2,2048]{2,1,0:T(2,128)(2,1)}), bf16[64,2,2048]{2,1,0:T(2,128)(2,1)}, u32[]{:S(2)}, u32[]{:S(2)}) %all-to-all-start.12) | async-done | bytes 524320 | tf_op jit(solution)/shard_map/all_to_all | solution.py:187
  454.4 5.9 all-to-all-start.13
  460.9 17.0 %all-to-all-done.13 = bf16[64,2,2048]{2,1,0:T(2,128)(2,1)} async-done(((bf16[64,2,2048]{2,1,0:T(2,128)(2,1)}), bf16[64,2,2048]{2,1,0:T(2,128)(2,1)}, u32[]{:S(2)}, u32[]{:S(2)}) %all-to-all-start.13) | async-done | bytes 524320 | tf_op jit(solution)/shard_map/all_to_all | solution.py:201
  485.7 9.2 collective-permute-done.5
  499.4 6.5 all-to-all-start.14
  513.6 9.7 all-to-all-done.14
  526.3 6.0 all-to-all-start.15
  534.6 15.3 %all-to-all-done.15 = bf16[64,2,2048]{2,1,0:T(2,128)(2,1)} async-done(((bf16[64,2,2048]{2,1,0:T(2,128)(2,1)}), bf16[64,2,2048]{2,1,0:T(2,128)(2,1)}, u32[]{:S(2)}, u32[]{:S(2)}) %all-to-all-start.15) | async-done | bytes 524320 | tf_op jit(solution)/shard_map/all_to_all | solution.py:201
  557.3 55.1 %collective-permute-done.6 = bf16[64,2048]{1,0:T(8,128)(2,1)} collective-permute-done((bf16[64,2048]{1,0:T(8,128)(2,1)}, bf16[64,2048]{1,0:T(8,128)(2,1)}, u32[]{:S(2)}, u32[]{:S(2)}) %collective-permute-start.6) | collective-permute-done | bytes 262176 | tf_op jit(solution)/shard_map/ppermute | solution.py:12
  616.9 6.1 all-to-all-start.16
  623.2 17.4 %all-to-all-done.16 = bf16[64,2,2048]{2,1,0:T(2,128)(2,1)} async-done(((bf16[64,2,2048]{2,1,0:T(2,128)(2,1)}), bf16[64,2,2048]{2,1,0:T(2,128)(2,1)}, u32[]{:S(2)}, u32[]{:S(2)}) %all-to-all-start.16) | async-done | bytes 524320 | tf_op jit(solution)/shard_map/all_to_all | solution.py:187
  640.6 15.8 %conditional.18 = (bf16[128,2048]{1,0:T(8,128)(2,1)}) conditional(s32[]{:T(128)} %convert_element_type.461, () %tuple.114, (bf16[64,2,2048]{2,1,0:T(2,128)(2,1)}, bf16[768,2048]{1,0:T(8,128)(2,1)}, f32[2,64,2,1536]{3,2,1,0:T(2,128)}, s32[]{:T(128)}, bf16[2048,1536]{1,0:T(8,128)(2,1)}) %tuple.238), branch_computations={%region_90.91_spmd, %region_91.92_spmd} | conditional | flops 1210286080 | bytes 16252940 | solution.py:198
  647.3 3.4 fusion.43
  650.7 5.7 convolution_convert_fusion.8
  658.6 5.9 all-to-all-start.17
  667.0 15.1 %all-to-all-done.17 = bf16[64,2,2048]{2,1,0:T(2,128)(2,1)} async-done(((bf16[64,2,2048]{2,1,0:T(2,128)(2,1)}), bf16[64,2,2048]{2,1,0:T(2,128)(2,1)}, u32[]{:S(2)}, u32[]{:S(2)}) %all-to-all-start.17) | async-done | bytes 524320 | tf_op jit(solution)/shard_map/all_to_all | solution.py:201
  690.4 6.9 collective-permute-done.7
  700.7 6.4 all-to-all-start.18
  710.0 14.7 %all-to-all-done.18 = bf16[64,2,2048]{2,1,0:T(2,128)(2,1)} async-done(((bf16[64,2,2048]{2,1,0:T(2,128)(2,1)}), bf16[64,2,2048]{2,1,0:T(2,128)(2,1)}, u32[]{:S(2)}, u32[]{:S(2)}) %all-to-all-start.18) | async-done | bytes 524320 | tf_op jit(solution)/shard_map/all_to_all | solution.py:187
  724.7 11.1 %conditional.19 = (bf16[128,2048]{1,0:T(8,128)(2,1)S(1)}) conditional(s32[]{:T(128)} %convert_element_type.473, () %tuple.116, (bf16[64,2,2048]{2,1,0:T(2,128)(2,1)}, bf16[768,2048]{1,0:T(8,128)(2,1)}, f32[2,64,2,1536]{3,2,1,0:T(2,128)}, s32[]{:T(128)}, bf16[2048,1536]{1,0:T(8,128)(2,1)}) %tuple.239), branch_computations={%region_102.103_spmd, %region_103.104_spmd} | conditional | flops 1210286080 | bytes 16252940 | solution.py:198
  727.7 3.1 fusion.50
  730.9 4.9 convolution_convert_fusion.9
  736.9 5.7 all-to-all-start.19
  745.0 182.3 %all-reduce.2.cloned.1.call-done = f32[2048,64]{0,1:T(8,128)} async-done(((f32[2048,64]{0,1:T(8,128)}), f32[2048,64]{0,1:T(8,128)}) %all-reduce.2.cloned.1.call-update) | async-done | bytes 524304 | tf_op jit(solution)/shard_map/psum | solution.py:225
  930.1 128.3 %psum.15 = f32[2048]{0:T(1024)S(1)} all-reduce(f32[2048]{0:T(1024)S(1)} %select_add_fusion), channel_id=1, replica_groups=mesh['section'=4,'expert'=64] {'expert'}, use_global_device_ids=true, to_apply=%region_114.115 | all-reduce | flops 2048 | bytes 16384 | tf_op jit(solution)/shard_map/psum | solution.py:225
  (410 shorter events, 201.3 us)
Async XLA Ops:
  7.2 21.9 %copy-start = (bf16[1,2048,64]{1,2,0:T(8,128)(2,1)S(1)}, bf16[1,2048,64]{1,2,0:T(8,128)(2,1)}, u32[]{:S(2)}) copy-start(bf16[1,2048,64]{1,2,0:T(8,128)(2,1)} %param.32) | copy-start | bytes 786436
  7.2 21.9 %copy-start.1 = (bf16[2,64,2048]{2,1,0:T(8,128)(2,1)S(1)}, bf16[2,64,2048]{2,1,0:T(8,128)(2,1)}, u32[]{:S(2)}) copy-start(bf16[2,64,2048]{2,1,0:T(8,128)(2,1)} %param.28) | copy-start | bytes 1572868
  7.2 21.9 %copy-start.11 = (f32[1,2048]{1,0:T(1,128)S(1)}, f32[1,2048]{1,0:T(1,128)}, u32[]{:S(2)}) copy-start(f32[1,2048]{1,0:T(1,128)} %param.31) | copy-start | bytes 24580
  8.8 425.2 %copy-start.27 = (s32[1,1,64,2]{2,3,1,0:T(2,128)}, s32[1,1,64,2]{2,3,1,0:T(2,128)S(1)}, u32[]{:S(2)}) copy-start(s32[1,1,64,2]{2,3,1,0:T(2,128)S(1)} %get-tuple-element.318) | copy-start | bytes 1540
  8.8 476.8 %copy-start.30 = (s32[1,1,64,2]{2,3,1,0:T(2,128)}, s32[1,1,64,2]{2,3,1,0:T(2,128)S(1)}, u32[]{:S(2)}) copy-start(s32[1,1,64,2]{2,3,1,0:T(2,128)S(1)} %get-tuple-element.319) | copy-start | bytes 1540
  15.9 30.8 %all-to-all-start = ((bf16[64,2,2048]{2,1,0:T(2,128)(2,1)}), bf16[64,2,2048]{2,1,0:T(2,128)(2,1)S(1)}, u32[]{:S(2)}, u32[]{:S(2)}) async-start(bf16[64,2,2048]{2,1,0:T(2,128)(2,1)} %reshape.765), calls=%async_computation | async-start | bytes 1048576 | tf_op jit(solution)/shard_map/all_to_all | solution.py:125
  53.7 26.2 %copy-start.12 = (f32[1,64,2,1536]{3,2,1,0:T(2,128)}, f32[1,64,2,1536]{3,2,1,0:T(2,128)S(1)}, u32[]{:S(2)}) copy-start(f32[1,64,2,1536]{3,2,1,0:T(2,128)S(1)} %get-tuple-element.232) | copy-start | bytes 2359300
  54.8 23.4 %all-to-all-start.1 = ((bf16[64,2,2048]{2,1,0:T(2,128)(2,1)}), bf16[64,2,2048]{2,1,0:T(2,128)(2,1)S(1)}, u32[]{:S(2)}, u32[]{:S(2)}) async-start(bf16[64,2,2048]{2,1,0:T(2,128)(2,1)} %reshape.766), calls=%async_computation.1 | async-start | bytes 1048576 | tf_op jit(solution)/shard_map/all_to_all | solution.py:140
  79.8 6.8 collective-permute-start
  86.9 60.7 %copy-start.5 = (bf16[64,2048]{1,0:T(8,128)(2,1)}, bf16[64,2048]{1,0:T(8,128)(2,1)S(1)}, u32[]{:S(2)}) copy-start(bf16[64,2048]{1,0:T(8,128)(2,1)S(1)} %get-tuple-element.307) | copy-start | bytes 786436
  88.4 24.0 %all-to-all-start.2 = ((bf16[64,2,2048]{2,1,0:T(2,128)(2,1)}), bf16[64,2,2048]{2,1,0:T(2,128)(2,1)S(1)}, u32[]{:S(2)}, u32[]{:S(2)}) async-start(bf16[64,2,2048]{2,1,0:T(2,128)(2,1)} %reshape.768), calls=%async_computation.2 | async-start | bytes 1048576 | tf_op jit(solution)/shard_map/all_to_all | solution.py:125
  120.2 27.4 %copy-start.14 = (f32[1,64,2,1536]{3,2,1,0:T(2,128)}, f32[1,64,2,1536]{3,2,1,0:T(2,128)S(1)}, u32[]{:S(2)}) copy-start(f32[1,64,2,1536]{3,2,1,0:T(2,128)S(1)} %get-tuple-element.233) | copy-start | bytes 2359300
  122.6 23.4 %all-to-all-start.3 = ((bf16[64,2,2048]{2,1,0:T(2,128)(2,1)}), bf16[64,2,2048]{2,1,0:T(2,128)(2,1)S(1)}, u32[]{:S(2)}, u32[]{:S(2)}) async-start(bf16[64,2,2048]{2,1,0:T(2,128)(2,1)} %reshape.769), calls=%async_computation.3 | async-start | bytes 1048576 | tf_op jit(solution)/shard_map/all_to_all | solution.py:140
  147.6 18.3 %copy-start.2 = (bf16[2,64,2048]{2,1,0:T(8,128)(2,1)S(1)}, bf16[2,64,2048]{2,1,0:T(8,128)(2,1)}, u32[]{:S(2)}) copy-start(bf16[2,64,2048]{2,1,0:T(8,128)(2,1)} %param.29) | copy-start | bytes 1572868
  147.7 9.5 collective-permute-start.1
  152.9 15.4 %copy-start.13 = (f32[1,64,2,1536]{3,2,1,0:T(2,128)S(1)}, f32[1,64,2,1536]{3,2,1,0:T(2,128)}, u32[]{:S(2)}) copy-start(f32[1,64,2,1536]{3,2,1,0:T(2,128)} %copy-done.12) | copy-start | bytes 2359300
  157.4 12.2 %copy-start.7 = (bf16[64,2048]{1,0:T(8,128)(2,1)}, bf16[64,2048]{1,0:T(8,128)(2,1)S(1)}, u32[]{:S(2)}) copy-start(bf16[64,2048]{1,0:T(8,128)(2,1)S(1)} %get-tuple-element.305) | copy-start | bytes 786436
  158.9 23.9 %all-to-all-start.4 = ((bf16[64,2,2048]{2,1,0:T(2,128)(2,1)}), bf16[64,2,2048]{2,1,0:T(2,128)(2,1)S(1)}, u32[]{:S(2)}, u32[]{:S(2)}) async-start(bf16[64,2,2048]{2,1,0:T(2,128)(2,1)} %reshape.771), calls=%async_computation.4 | async-start | bytes 1048576 | tf_op jit(solution)/shard_map/all_to_all | solution.py:125
  184.2 23.7 %all-to-all-start.5 = ((bf16[64,2,2048]{2,1,0:T(2,128)(2,1)}), bf16[64,2,2048]{2,1,0:T(2,128)(2,1)}, u32[]{:S(2)}, u32[]{:S(2)}) async-start(bf16[64,2,2048]{2,1,0:T(2,128)(2,1)} %reshape.772), calls=%async_computation.5 | async-start | bytes 1048576 | tf_op jit(solution)/shard_map/all_to_all | solution.py:140
  209.9 14.3 %copy-start.6 = (bf16[64,2048]{1,0:T(8,128)(2,1)S(1)}, bf16[64,2048]{1,0:T(8,128)(2,1)}, u32[]{:S(2)}) copy-start(bf16[64,2048]{1,0:T(8,128)(2,1)} %copy-done.5) | copy-start | bytes 786436
  209.9 14.3 %copy-start.19 = (bf16[1,64,2048]{2,1,0:T(8,128)(2,1)S(1)}, bf16[1,64,2048]{2,1,0:T(8,128)(2,1)}, u32[]{:S(2)}) copy-start(bf16[1,64,2048]{2,1,0:T(8,128)(2,1)} %constant_dynamic-slice_fusion.33) | copy-start | bytes 786436
  213.3 16.0 %collective-permute-start.2 = (bf16[64,2048]{1,0:T(8,128)(2,1)S(1)}, bf16[64,2048]{1,0:T(8,128)(2,1)S(1)}, u32[]{:S(2)}, u32[]{:S(2)}) collective-permute-start(bf16[64,2048]{1,0:T(8,128)(2,1)S(1)} %fusion.170), channel_id=1, source_target_pairs={{0,64},{64,128},{128,192},{1,65},{65,129},{129,193},{2,66},{66,130... | collective-permute-start | bytes 786440 | tf_op jit(solution)/shard_map/ppermute | solution.py:12
  233.6 24.0 %all-to-all-start.6 = ((bf16[64,2,2048]{2,1,0:T(2,128)(2,1)}), bf16[64,2,2048]{2,1,0:T(2,128)(2,1)}, u32[]{:S(2)}, u32[]{:S(2)}) async-start(bf16[64,2,2048]{2,1,0:T(2,128)(2,1)} %reshape.774), calls=%async_computation.6 | async-start | bytes 1048576 | tf_op jit(solution)/shard_map/all_to_all | solution.py:125
  261.7 23.5 %all-to-all-start.7 = ((bf16[64,2,2048]{2,1,0:T(2,128)(2,1)}), bf16[64,2,2048]{2,1,0:T(2,128)(2,1)}, u32[]{:S(2)}, u32[]{:S(2)}) async-start(bf16[64,2,2048]{2,1,0:T(2,128)(2,1)} %reshape.775), calls=%async_computation.7 | async-start | bytes 1048576 | tf_op jit(solution)/shard_map/all_to_all | solution.py:140
  290.7 9.4 collective-permute-start.3
  302.5 23.9 %all-to-all-start.9 = ((bf16[64,2,2048]{2,1,0:T(2,128)(2,1)}), bf16[64,2,2048]{2,1,0:T(2,128)(2,1)S(1)}, u32[]{:S(2)}, u32[]{:S(2)}) async-start(bf16[64,2,2048]{2,1,0:T(2,128)(2,1)} %reshape.778), calls=%async_computation.9 | async-start | bytes 1048576 | tf_op jit(solution)/shard_map/all_to_all | solution.py:125
  309.9 92.8 %copy-start.43 = (f32[64]{0:T(128)}, f32[64]{0:T(128)S(1)}, u32[]{:S(2)}) copy-start(f32[64]{0:T(128)S(1)} %add_rsqrt_fusion.5) | copy-start | bytes 772
  326.4 23.7 %all-to-all-start.8 = ((bf16[64,2,2048]{2,1,0:T(2,128)(2,1)}), bf16[64,2,2048]{2,1,0:T(2,128)(2,1)}, u32[]{:S(2)}, u32[]{:S(2)}) async-start(bf16[64,2,2048]{2,1,0:T(2,128)(2,1)} %reshape.777), calls=%async_computation.8 | async-start | bytes 1048576 | tf_op jit(solution)/shard_map/all_to_all | solution.py:187
  350.1 23.4 %all-to-all-start.11 = ((bf16[64,2,2048]{2,1,0:T(2,128)(2,1)}), bf16[64,2,2048]{2,1,0:T(2,128)(2,1)S(1)}, u32[]{:S(2)}, u32[]{:S(2)}) async-start(bf16[64,2,2048]{2,1,0:T(2,128)(2,1)} %reshape.781), calls=%async_computation.11 | async-start | bytes 1048576 | tf_op jit(solution)/shard_map/all_to_all | solution.py:140
  373.5 23.9 %all-to-all-start.10 = ((bf16[64,2,2048]{2,1,0:T(2,128)(2,1)}), bf16[64,2,2048]{2,1,0:T(2,128)(2,1)}, u32[]{:S(2)}, u32[]{:S(2)}) async-start(bf16[64,2,2048]{2,1,0:T(2,128)(2,1)} %reshape.779), calls=%async_computation.10 | async-start | bytes 1048576 | tf_op jit(solution)/shard_map/all_to_all | solution.py:201
  383.8 19.0 %copy-start.3 = (bf16[2,64,2048]{2,1,0:T(8,128)(2,1)S(1)}, bf16[2,64,2048]{2,1,0:T(8,128)(2,1)}, u32[]{:S(2)}) copy-start(bf16[2,64,2048]{2,1,0:T(8,128)(2,1)} %param.29) | copy-start | bytes 1572868
  385.2 18.6 %copy-start.24 = (bf16[64,64]{1,0:T(8,128)(2,1)}, bf16[64,64]{1,0:T(8,128)(2,1)S(1)}, u32[]{:S(2)}) copy-start(bf16[64,64]{1,0:T(8,128)(2,1)S(1)} %select_reduce_fusion.16) | copy-start | bytes 24580
  403.7 19.5 %collective-permute-start.4 = (bf16[64,2048]{1,0:T(8,128)(2,1)}, bf16[64,2048]{1,0:T(8,128)(2,1)}, u32[]{:S(2)}, u32[]{:S(2)}) collective-permute-start(bf16[64,2048]{1,0:T(8,128)(2,1)} %get-tuple-element.297), channel_id=1, source_target_pairs={{64,0},{128,64},{192,128},{65,1},{129,65},{193,129},{66,2},{130,66... | collective-permute-start | bytes 786440 | tf_op jit(solution)/shard_map/ppermute | solution.py:12
  405.0 77.2 %copy-start.36 = (f32[64]{0:T(128)}, f32[64]{0:T(128)S(1)}, u32[]{:S(2)}) copy-start(f32[64]{0:T(128)S(1)} %add_rsqrt_fusion.3) | copy-start | bytes 772
  427.7 23.7 %all-to-all-start.12 = ((bf16[64,2,2048]{2,1,0:T(2,128)(2,1)}), bf16[64,2,2048]{2,1,0:T(2,128)(2,1)}, u32[]{:S(2)}, u32[]{:S(2)}) async-start(bf16[64,2,2048]{2,1,0:T(2,128)(2,1)} %reshape.783), calls=%async_computation.12 | async-start | bytes 1048576 | tf_op jit(solution)/shard_map/all_to_all | solution.py:187
  434.0 62.0 %copy-start.32 = (s32[2,64]{1,0:T(2,128)}, s32[2,64]{1,0:T(2,128)S(1)}, u32[]{:S(2)}) copy-start(s32[2,64]{1,0:T(2,128)S(1)} %copy.128) | copy-start | bytes 1540
  454.4 23.5 %all-to-all-start.13 = ((bf16[64,2,2048]{2,1,0:T(2,128)(2,1)}), bf16[64,2,2048]{2,1,0:T(2,128)(2,1)}, u32[]{:S(2)}, u32[]{:S(2)}) async-start(bf16[64,2,2048]{2,1,0:T(2,128)(2,1)} %reshape.784), calls=%async_computation.13 | async-start | bytes 1048576 | tf_op jit(solution)/shard_map/all_to_all | solution.py:201
  460.3 23.9 %copy-start.38 = (f32[64]{0:T(128)}, f32[64]{0:T(128)S(1)}, u32[]{:S(2)}) copy-start(f32[64]{0:T(128)S(1)} %add_rsqrt_fusion.2) | copy-start | bytes 772
  460.9 35.1 %copy-start.22 = (bf16[64,64]{1,0:T(8,128)(2,1)}, bf16[64,64]{1,0:T(8,128)(2,1)S(1)}, u32[]{:S(2)}) copy-start(bf16[64,64]{1,0:T(8,128)(2,1)S(1)} %select_reduce_fusion.12) | copy-start | bytes 24580
  482.3 23.6 %copy-start.40 = (s32[128]{0:T(128)S(1)}, s32[128]{0:T(128)}, u32[]{:S(2)}) copy-start(s32[128]{0:T(128)} %eq.414) | copy-start | bytes 1540
  484.2 10.7 %collective-permute-start.5 = (bf16[64,2048]{1,0:T(8,128)(2,1)}, bf16[64,2048]{1,0:T(8,128)(2,1)}, u32[]{:S(2)}, u32[]{:S(2)}) collective-permute-start(bf16[64,2048]{1,0:T(8,128)(2,1)} %get-tuple-element.293), channel_id=1, source_target_pairs={{64,0},{128,64},{192,128},{65,1},{129,65},{193,129},{66,2},{130,66... | collective-permute-start | bytes 786440 | tf_op jit(solution)/shard_map/ppermute | solution.py:12
  485.7 20.2 %copy-start.34 = (f32[64,2]{0,1:T(2,128)}, f32[64,2]{0,1:T(2,128)S(1)}, u32[]{:S(2)}) copy-start(f32[64,2]{0,1:T(2,128)S(1)} %add_divide_fusion.7) | copy-start | bytes 1540
  499.4 23.9 %all-to-all-start.14 = ((bf16[64,2,2048]{2,1,0:T(2,128)(2,1)}), bf16[64,2,2048]{2,1,0:T(2,128)(2,1)}, u32[]{:S(2)}, u32[]{:S(2)}) async-start(bf16[64,2,2048]{2,1,0:T(2,128)(2,1)} %reshape.786), calls=%async_computation.14 | async-start | bytes 1048576 | tf_op jit(solution)/shard_map/all_to_all | solution.py:187
  524.1 10.4 copy-start.31
  524.2 27.9 %copy-start.33 = (s32[2,64]{1,0:T(2,128)S(1)}, s32[2,64]{1,0:T(2,128)}, u32[]{:S(2)}) copy-start(s32[2,64]{1,0:T(2,128)} %copy-done.32) | copy-start | bytes 1540
  526.3 27.1 %copy-start.39 = (f32[64]{0:T(128)S(1)}, f32[64]{0:T(128)}, u32[]{:S(2)}) copy-start(f32[64]{0:T(128)} %copy-done.38) | copy-start | bytes 772
  526.3 23.6 %all-to-all-start.15 = ((bf16[64,2,2048]{2,1,0:T(2,128)(2,1)}), bf16[64,2,2048]{2,1,0:T(2,128)(2,1)}, u32[]{:S(2)}, u32[]{:S(2)}) async-start(bf16[64,2,2048]{2,1,0:T(2,128)(2,1)} %reshape.787), calls=%async_computation.15 | async-start | bytes 1048576 | tf_op jit(solution)/shard_map/all_to_all | solution.py:201
  534.5 22.6 %copy-start.29 = (s32[1,1,64,2]{2,3,1,0:T(2,128)S(1)}, s32[1,1,64,2]{2,3,1,0:T(2,128)}, u32[]{:S(2)}) copy-start(s32[1,1,64,2]{2,3,1,0:T(2,128)} %get-tuple-element.327) | copy-start | bytes 1540
  553.8 69.4 %copy-start.45 = (f32[64]{0:T(128)S(1)}, f32[64]{0:T(128)}, u32[]{:S(2)}) copy-start(f32[64]{0:T(128)} %get-tuple-element.248) | copy-start | bytes 772
  555.8 56.6 %collective-permute-start.6 = (bf16[64,2048]{1,0:T(8,128)(2,1)}, bf16[64,2048]{1,0:T(8,128)(2,1)}, u32[]{:S(2)}, u32[]{:S(2)}) collective-permute-start(bf16[64,2048]{1,0:T(8,128)(2,1)} %get-tuple-element.289), channel_id=1, source_target_pairs={{64,0},{128,64},{192,128},{65,1},{129,65},{193,129},{66,2},{130,66... | collective-permute-start | bytes 786440 | tf_op jit(solution)/shard_map/ppermute | solution.py:12
  616.9 23.7 %all-to-all-start.16 = ((bf16[64,2,2048]{2,1,0:T(2,128)(2,1)}), bf16[64,2,2048]{2,1,0:T(2,128)(2,1)}, u32[]{:S(2)}, u32[]{:S(2)}) async-start(bf16[64,2,2048]{2,1,0:T(2,128)(2,1)} %reshape.789), calls=%async_computation.16 | async-start | bytes 1048576 | tf_op jit(solution)/shard_map/all_to_all | solution.py:187
  640.6 24.2 %copy-start.28 = (s32[1,1,64,2]{2,3,1,0:T(2,128)S(1)}, s32[1,1,64,2]{2,3,1,0:T(2,128)}, u32[]{:S(2)}) copy-start(s32[1,1,64,2]{2,3,1,0:T(2,128)} %copy-done.27) | copy-start | bytes 1540
  658.6 23.5 %all-to-all-start.17 = ((bf16[64,2,2048]{2,1,0:T(2,128)(2,1)}), bf16[64,2,2048]{2,1,0:T(2,128)(2,1)}, u32[]{:S(2)}, u32[]{:S(2)}) async-start(bf16[64,2,2048]{2,1,0:T(2,128)(2,1)} %reshape.790), calls=%async_computation.17 | async-start | bytes 1048576 | tf_op jit(solution)/shard_map/all_to_all | solution.py:201
  666.8 22.4 %copy-start.25 = (bf16[64,64]{1,0:T(8,128)(2,1)S(1)}, bf16[64,64]{1,0:T(8,128)(2,1)}, u32[]{:S(2)}) copy-start(bf16[64,64]{1,0:T(8,128)(2,1)} %copy-done.24) | copy-start | bytes 24580
  666.8 22.4 %copy-start.44 = (f32[64]{0:T(128)S(1)}, f32[64]{0:T(128)}, u32[]{:S(2)}) copy-start(f32[64]{0:T(128)} %copy-done.43) | copy-start | bytes 772
  684.1 13.1 %copy-start.4 = (bf16[2,64,2048]{2,1,0:T(8,128)(2,1)S(1)}, bf16[2,64,2048]{2,1,0:T(8,128)(2,1)}, u32[]{:S(2)}) copy-start(bf16[2,64,2048]{2,1,0:T(8,128)(2,1)} %param.29) | copy-start | bytes 1572868
  686.0 21.1 %copy-start.23 = (bf16[64,64]{1,0:T(8,128)(2,1)S(1)}, bf16[64,64]{1,0:T(8,128)(2,1)}, u32[]{:S(2)}) copy-start(bf16[64,64]{1,0:T(8,128)(2,1)} %copy-done.22) | copy-start | bytes 24580
  686.0 21.1 %copy-start.37 = (f32[64]{0:T(128)S(1)}, f32[64]{0:T(128)}, u32[]{:S(2)}) copy-start(f32[64]{0:T(128)} %copy-done.36) | copy-start | bytes 772
  687.9 9.4 collective-permute-start.7
  700.7 24.0 %all-to-all-start.18 = ((bf16[64,2,2048]{2,1,0:T(2,128)(2,1)}), bf16[64,2,2048]{2,1,0:T(2,128)(2,1)}, u32[]{:S(2)}, u32[]{:S(2)}) async-start(bf16[64,2,2048]{2,1,0:T(2,128)(2,1)} %reshape.792), calls=%async_computation.18 | async-start | bytes 1048576 | tf_op jit(solution)/shard_map/all_to_all | solution.py:187
  724.7 18.1 %copy-start.18 = (f32[2048,64]{0,1:T(8,128)S(1)}, f32[2048,64]{0,1:T(8,128)}, u32[]{:S(2)}) copy-start(f32[2048,64]{0,1:T(8,128)} %fusion.63) | copy-start | bytes 1572868
  736.9 192.2 %all-to-all-start.19 = ((bf16[64,2,2048]{2,1,0:T(2,128)(2,1)}), bf16[64,2,2048]{2,1,0:T(2,128)(2,1)S(1)}, u32[]{:S(2)}, u32[]{:S(2)}) async-start(bf16[64,2,2048]{2,1,0:T(2,128)(2,1)} %reshape.793), calls=%async_computation.19 | async-start | bytes 1048576 | tf_op jit(solution)/shard_map/all_to_all | solution.py:201
  742.6 184.7 %all-reduce.2.cloned.1.call-start = ((), (), s32[]{:S(2)}) async-start(), calls=%async_computation.20 | async-start | bytes 1048576 | tf_op jit(solution)/shard_map/psum | solution.py:225
  743.9 186.2 %copy-start.26 = (f32[2048]{0:T(1024)S(1)}, f32[2048]{0:T(1024)}, u32[]{:S(2)}) copy-start(f32[2048]{0:T(1024)} %get-tuple-element.240) | copy-start | bytes 24580
  (10 other events, 39.0 us)
Sparse Core Ops, SparseCore 0:
  747.5 179.7 all-reduce.1
where the time goes:
time: 1080 us; the launch traced here: 1070 us
  waiting for transfers between devices  551 us (51%)
  starting transfers between devices  154 us (14%)
  blocking collectives  128 us (12%)
  local copies, waits for them, and re-layouts  98.3 us (9%)
  matrix products  68 us (6%)
  other arithmetic  52.6 us (5%)
  between operations  15.8 us (1%)
    psum x1, waiting for transfers between devices, local(): router_sum, gain_sum = lax.psum((router_total, gain_total), 'expert')  182 us
    psum x1, blocking collectives, local(): router_sum, gain_sum = lax.psum((router_total, gain_total), 'expert')  128 us
    ppermute x8, waiting for transfers between devices, shifted(): return lax.ppermute(block, axis, route)  107 us
    all_to_all x5, waiting for transfers between devices, local(): lax.all_to_all(run_result.reshape(row_shape), 'expert', split_axis=0, con...  69.7 us
    all_to_all x5, waiting for transfers between devices, local(): lax.all_to_all(outgoing, 'expert', split_axis=0, concat_axis=0, tiled=True)  68 us
    all_to_all x5, waiting for transfers between devices, local(): lax.all_to_all(grad_send, 'expert', split_axis=0, concat_axis=0, tiled=True)  64.5 us
    all_to_all x5, waiting for transfers between devices, local(): lax.all_to_all(result.reshape(received.shape), 'expert', split_axis=0, co...  59.6 us
    all_to_all x5, starting transfers between devices, local(): lax.all_to_all(outgoing, 'expert', split_axis=0, concat_axis=0, tiled=True)  38.4 us
  transfers between devices with their start and end apart: 29, of which 28 were waited for; matrix products, arithmetic and copies ran while one was open for 8% of the time, Pallas kernels for 0%

commit v1 on v0

--- a/solution.py
+++ b/solution.py
@@ -222,7 +222,16 @@
         gain_total = gain_total + jnp.where(working, jnp.sum(normed_grad * centred, axis=0), 0.0)
         grads_out = store_at(grads_out, leaving, clipped, inside)
         inbox_rows = shifted(leaving, "section", -1)
-    router_sum, gain_sum = lax.psum((router_total, gain_total), "expert")
+    owners = lax.axis_size("expert")
+    pieces = jnp.concatenate(
+        [router_total.reshape(owners, -1), gain_total.reshape(owners, -1)], axis=1
+    )
+    pieces = lax.all_to_all(pieces, "expert", split_axis=0, concat_axis=0, tiled=True)
+    piece = jnp.broadcast_to(jnp.sum(pieces, axis=0)[None], pieces.shape)
+    pieces = lax.all_to_all(piece, "expert", split_axis=0, concat_axis=0, tiled=True)
+    split = model_width * experts // owners
+    router_sum = pieces[:, :split].reshape(model_width, experts)
+    gain_sum = pieces[:, split:].reshape(model_width)
     denominator = micro_count * choice_count * tokens_here
     return (grads_out[None], (router_sum / denominator)[None], (gain_sum / denominator)[None])
 

time: 1080 us -> 828 us (0.77)
  waiting for transfers between devices: 551 us -> 400 us
  blocking collectives: 128 us -> 24.1 us
  between operations: 15.8 us -> 2.66 us
    psum x1 -> x0, waiting for transfers between devices: 182 us -> none  [local(): router_sum, gain_sum = lax.psum((router_total, gain_total), 'expert')]
    psum x1 -> x0, blocking collectives: 128 us -> none  [local(): router_sum, gain_sum = lax.psum((router_total, gain_total), 'expert')]
    all_to_all x0 -> x1, blocking collectives: none -> 24.1 us  [local(): lax.all_to_all(pieces, 'expert', split_axis=0, concat_axis=0, tiled=True)]
    all_to_all x0 -> x1, waiting for transfers between devices: none -> 15.3 us  [local(): lax.all_to_all(piece, 'expert', split_axis=0, concat_axis=0, tiled=True)]
    all_to_all x5, waiting for transfers between devices: 59.6 us -> 74.8 us  [local(): lax.all_to_all(result.reshape(received.shape), 'expert', split_axis=0, co...]
  transfers between devices with their start and end apart: 29 -> 29, of which waited for: 28 -> 29; matrix products, arithmetic and copies ran while one was open for 8% -> 10% of each run, Pallas kernels for 0% -> 0%
where the time goes in v1:
time: 828 us; the launch traced here: 816 us
  waiting for transfers between devices  400 us (48%)
  starting transfers between devices  160 us (19%)
  local copies, waits for them, and re-layouts  109 us (13%)
  matrix products  68.8 us (8%)
  other arithmetic  51.7 us (6%)
  blocking collectives  24.1 us (3%)
    ppermute x8, waiting for transfers between devices, shifted(): return lax.ppermute(block, axis, route)  108 us
    all_to_all x5, waiting for transfers between devices, local(): lax.all_to_all(result.reshape(received.shape), 'expert', split_axis=0, co...  74.8 us
    all_to_all x5, waiting for transfers between devices, local(): lax.all_to_all(run_result.reshape(row_shape), 'expert', split_axis=0, con...  69.7 us
    all_to_all x5, waiting for transfers between devices, local(): lax.all_to_all(outgoing, 'expert', split_axis=0, concat_axis=0, tiled=True)  68 us
    all_to_all x5, waiting for transfers between devices, local(): lax.all_to_all(grad_send, 'expert', split_axis=0, concat_axis=0, tiled=True)  64.3 us
    all_to_all x5, starting transfers between devices, local(): lax.all_to_all(outgoing, 'expert', split_axis=0, concat_axis=0, tiled=True)  38.4 us
    all_to_all x5, starting transfers between devices, local(): lax.all_to_all(grad_send, 'expert', split_axis=0, concat_axis=0, tiled=True)  31.1 us
    all_to_all x5, starting transfers between devices, local(): lax.all_to_all(result.reshape(received.shape), 'expert', split_axis=0, co...  30.1 us
  transfers between devices with their start and end apart: 29, of which 29 were waited for; matrix products, arithmetic and copies ran while one was open for 10% of the time, Pallas kernels for 0%

profile of v1, /device:TPU:1, one launch (start us, length us, event | category | flops | bytes accessed | tf_op | source)
XLA Modules:
  0.0 816.1 jit_solution(6485836800646226988)
XLA Ops:
  9.4 13.1 %all-to-all-start = ((bf16[64,2,2048]{2,1,0:T(2,128)(2,1)}), bf16[64,2,2048]{2,1,0:T(2,128)(2,1)S(1)}, u32[]{:S(2)}, u32[]{:S(2)}) async-start(bf16[64,2,2048]{2,1,0:T(2,128)(2,1)} %reshape.826), calls=%async_computation | async-start | bytes 1048576 | tf_op jit(solution)/shard_map/all_to_all | solution.py:125
  23.7 16.5 %all-to-all-done = bf16[64,2,2048]{2,1,0:T(2,128)(2,1)S(1)} async-done(((bf16[64,2,2048]{2,1,0:T(2,128)(2,1)}), bf16[64,2,2048]{2,1,0:T(2,128)(2,1)S(1)}, u32[]{:S(2)}, u32[]{:S(2)}) %all-to-all-start) | async-done | bytes 524320 | tf_op jit(solution)/shard_map/all_to_all | solution.py:125
  40.2 6.9 conditional.10
  40.4 3.8 fusion.376
  48.3 5.7 all-to-all-start.1
  56.0 15.6 %all-to-all-done.1 = bf16[64,2,2048]{2,1,0:T(2,128)(2,1)S(1)} async-done(((bf16[64,2,2048]{2,1,0:T(2,128)(2,1)}), bf16[64,2,2048]{2,1,0:T(2,128)(2,1)S(1)}, u32[]{:S(2)}, u32[]{:S(2)}) %all-to-all-start.1) | async-done | bytes 524320 | tf_op jit(solution)/shard_map/all_to_all | solution.py:140
  75.3 4.8 collective-permute-done
  81.8 6.5 all-to-all-start.2
  91.3 14.6 %all-to-all-done.2 = bf16[64,2,2048]{2,1,0:T(2,128)(2,1)S(1)} async-done(((bf16[64,2,2048]{2,1,0:T(2,128)(2,1)}), bf16[64,2,2048]{2,1,0:T(2,128)(2,1)S(1)}, u32[]{:S(2)}, u32[]{:S(2)}) %all-to-all-start.2) | async-done | bytes 524320 | tf_op jit(solution)/shard_map/all_to_all | solution.py:125
  105.9 7.7 conditional.11
  106.1 3.8 fusion.377
  116.1 5.7 all-to-all-start.3
  122.6 16.9 %all-to-all-done.3 = bf16[64,2,2048]{2,1,0:T(2,128)(2,1)S(1)} async-done(((bf16[64,2,2048]{2,1,0:T(2,128)(2,1)}), bf16[64,2,2048]{2,1,0:T(2,128)(2,1)S(1)}, u32[]{:S(2)}, u32[]{:S(2)}) %all-to-all-start.3) | async-done | bytes 524320 | tf_op jit(solution)/shard_map/all_to_all | solution.py:140
  141.1 4.3 collective-permute-start.1
  146.3 4.3 collective-permute-done.1
  152.3 6.2 all-to-all-start.4
  163.0 13.2 %all-to-all-done.4 = bf16[64,2,2048]{2,1,0:T(2,128)(2,1)S(1)} async-done(((bf16[64,2,2048]{2,1,0:T(2,128)(2,1)}), bf16[64,2,2048]{2,1,0:T(2,128)(2,1)S(1)}, u32[]{:S(2)}, u32[]{:S(2)}) %all-to-all-start.4) | async-done | bytes 524320 | tf_op jit(solution)/shard_map/all_to_all | solution.py:125
  177.6 6.0 all-to-all-start.5
  186.9 14.4 %all-to-all-done.5 = bf16[64,2,2048]{2,1,0:T(2,128)(2,1)} async-done(((bf16[64,2,2048]{2,1,0:T(2,128)(2,1)}), bf16[64,2,2048]{2,1,0:T(2,128)(2,1)}, u32[]{:S(2)}, u32[]{:S(2)}) %all-to-all-start.5) | async-done | bytes 524320 | tf_op jit(solution)/shard_map/all_to_all | solution.py:140
  206.8 10.8 %collective-permute-start.2 = (bf16[64,2048]{1,0:T(8,128)(2,1)S(1)}, bf16[64,2048]{1,0:T(8,128)(2,1)S(1)}, u32[]{:S(2)}, u32[]{:S(2)}) collective-permute-start(bf16[64,2048]{1,0:T(8,128)(2,1)S(1)} %fusion.170), channel_id=1, source_target_pairs={{0,64},{64,128},{128,192},{1,65},{65,129},{129,193},{2,66},{66,130... | collective-permute-start | bytes 786440 | tf_op jit(solution)/shard_map/ppermute | solution.py:12
  218.4 4.4 collective-permute-done.2
  227.0 6.4 all-to-all-start.6
  238.9 12.1 %all-to-all-done.6 = bf16[64,2,2048]{2,1,0:T(2,128)(2,1)} async-done(((bf16[64,2,2048]{2,1,0:T(2,128)(2,1)}), bf16[64,2,2048]{2,1,0:T(2,128)(2,1)}, u32[]{:S(2)}, u32[]{:S(2)}) %all-to-all-start.6) | async-done | bytes 524320 | tf_op jit(solution)/shard_map/all_to_all | solution.py:125
  255.2 5.9 all-to-all-start.7
  264.3 14.4 %all-to-all-done.7 = bf16[64,2,2048]{2,1,0:T(2,128)(2,1)} async-done(((bf16[64,2,2048]{2,1,0:T(2,128)(2,1)}), bf16[64,2,2048]{2,1,0:T(2,128)(2,1)}, u32[]{:S(2)}, u32[]{:S(2)}) %all-to-all-start.7) | async-done | bytes 524320 | tf_op jit(solution)/shard_map/all_to_all | solution.py:140
  284.2 4.1 collective-permute-start.3
  289.1 4.4 collective-permute-done.3
  296.0 6.2 all-to-all-start.9
  308.3 11.6 %all-to-all-done.9 = bf16[64,2,2048]{2,1,0:T(2,128)(2,1)S(1)} async-done(((bf16[64,2,2048]{2,1,0:T(2,128)(2,1)}), bf16[64,2,2048]{2,1,0:T(2,128)(2,1)S(1)}, u32[]{:S(2)}, u32[]{:S(2)}) %all-to-all-start.9) | async-done | bytes 524320 | tf_op jit(solution)/shard_map/all_to_all | solution.py:125
  319.9 6.1 all-to-all-start.8
  335.0 8.6 %all-to-all-done.8 = bf16[64,2,2048]{2,1,0:T(2,128)(2,1)} async-done(((bf16[64,2,2048]{2,1,0:T(2,128)(2,1)}), bf16[64,2,2048]{2,1,0:T(2,128)(2,1)}, u32[]{:S(2)}, u32[]{:S(2)}) %all-to-all-start.8) | async-done | bytes 524320 | tf_op jit(solution)/shard_map/all_to_all | solution.py:187
  343.6 5.7 all-to-all-start.11
  358.6 8.4 %all-to-all-done.11 = bf16[64,2,2048]{2,1,0:T(2,128)(2,1)S(1)} async-done(((bf16[64,2,2048]{2,1,0:T(2,128)(2,1)}), bf16[64,2,2048]{2,1,0:T(2,128)(2,1)S(1)}, u32[]{:S(2)}, u32[]{:S(2)}) %all-to-all-start.11) | async-done | bytes 524320 | tf_op jit(solution)/shard_map/all_to_all | solution.py:140
  366.9 6.5 all-to-all-start.10
  378.6 12.2 %all-to-all-done.10 = bf16[64,2,2048]{2,1,0:T(2,128)(2,1)} async-done(((bf16[64,2,2048]{2,1,0:T(2,128)(2,1)}), bf16[64,2,2048]{2,1,0:T(2,128)(2,1)}, u32[]{:S(2)}, u32[]{:S(2)}) %all-to-all-start.10) | async-done | bytes 524320 | tf_op jit(solution)/shard_map/all_to_all | solution.py:201
  399.0 17.7 %collective-permute-done.4 = bf16[64,2048]{1,0:T(8,128)(2,1)} collective-permute-done((bf16[64,2048]{1,0:T(8,128)(2,1)}, bf16[64,2048]{1,0:T(8,128)(2,1)}, u32[]{:S(2)}, u32[]{:S(2)}) %collective-permute-start.4) | collective-permute-done | bytes 262176 | tf_op jit(solution)/shard_map/ppermute | solution.py:12
  421.1 6.1 all-to-all-start.12
  430.7 14.1 %all-to-all-done.12 = bf16[64,2,2048]{2,1,0:T(2,128)(2,1)} async-done(((bf16[64,2,2048]{2,1,0:T(2,128)(2,1)}), bf16[64,2,2048]{2,1,0:T(2,128)(2,1)}, u32[]{:S(2)}, u32[]{:S(2)}) %all-to-all-start.12) | async-done | bytes 524320 | tf_op jit(solution)/shard_map/all_to_all | solution.py:187
  447.9 5.9 all-to-all-start.13
  454.4 17.0 %all-to-all-done.13 = bf16[64,2,2048]{2,1,0:T(2,128)(2,1)} async-done(((bf16[64,2,2048]{2,1,0:T(2,128)(2,1)}), bf16[64,2,2048]{2,1,0:T(2,128)(2,1)}, u32[]{:S(2)}, u32[]{:S(2)}) %all-to-all-start.13) | async-done | bytes 524320 | tf_op jit(solution)/shard_map/all_to_all | solution.py:201
  479.2 9.2 %collective-permute-done.5 = bf16[64,2048]{1,0:T(8,128)(2,1)} collective-permute-done((bf16[64,2048]{1,0:T(8,128)(2,1)}, bf16[64,2048]{1,0:T(8,128)(2,1)}, u32[]{:S(2)}, u32[]{:S(2)}) %collective-permute-start.5) | collective-permute-done | bytes 262176 | tf_op jit(solution)/shard_map/ppermute | solution.py:12
  492.9 6.5 all-to-all-start.14
  507.1 9.7 %all-to-all-done.14 = bf16[64,2,2048]{2,1,0:T(2,128)(2,1)} async-done(((bf16[64,2,2048]{2,1,0:T(2,128)(2,1)}), bf16[64,2,2048]{2,1,0:T(2,128)(2,1)}, u32[]{:S(2)}, u32[]{:S(2)}) %all-to-all-start.14) | async-done | bytes 524320 | tf_op jit(solution)/shard_map/all_to_all | solution.py:187
  519.8 6.0 all-to-all-start.15
  528.1 15.3 %all-to-all-done.15 = bf16[64,2,2048]{2,1,0:T(2,128)(2,1)} async-done(((bf16[64,2,2048]{2,1,0:T(2,128)(2,1)}), bf16[64,2,2048]{2,1,0:T(2,128)(2,1)}, u32[]{:S(2)}, u32[]{:S(2)}) %all-to-all-start.15) | async-done | bytes 524320 | tf_op jit(solution)/shard_map/all_to_all | solution.py:201
  550.8 55.1 %collective-permute-done.6 = bf16[64,2048]{1,0:T(8,128)(2,1)} collective-permute-done((bf16[64,2048]{1,0:T(8,128)(2,1)}, bf16[64,2048]{1,0:T(8,128)(2,1)}, u32[]{:S(2)}, u32[]{:S(2)}) %collective-permute-start.6) | collective-permute-done | bytes 262176 | tf_op jit(solution)/shard_map/ppermute | solution.py:12
  610.3 6.1 all-to-all-start.16
  616.7 17.4 %all-to-all-done.16 = bf16[64,2,2048]{2,1,0:T(2,128)(2,1)} async-done(((bf16[64,2,2048]{2,1,0:T(2,128)(2,1)}), bf16[64,2,2048]{2,1,0:T(2,128)(2,1)}, u32[]{:S(2)}, u32[]{:S(2)}) %all-to-all-start.16) | async-done | bytes 524320 | tf_op jit(solution)/shard_map/all_to_all | solution.py:187
  634.1 15.8 %conditional.18 = (bf16[128,2048]{1,0:T(8,128)(2,1)}) conditional(s32[]{:T(128)} %convert_element_type.461, () %tuple.114, (bf16[64,2,2048]{2,1,0:T(2,128)(2,1)}, bf16[768,2048]{1,0:T(8,128)(2,1)}, f32[2,64,2,1536]{3,2,1,0:T(2,128)}, s32[]{:T(128)}, bf16[2048,1536]{1,0:T(8,128)(2,1)}) %tuple.239), branch_computations={%region_90.91_spmd, %region_91.92_spmd} | conditional | flops 1210286080 | bytes 16252940 | solution.py:198
  640.7 3.4 fusion.43
  644.2 5.7 convolution_convert_fusion.8
  652.1 5.9 all-to-all-start.17
  660.2 15.3 %all-to-all-done.17 = bf16[64,2,2048]{2,1,0:T(2,128)(2,1)} async-done(((bf16[64,2,2048]{2,1,0:T(2,128)(2,1)}), bf16[64,2,2048]{2,1,0:T(2,128)(2,1)}, u32[]{:S(2)}, u32[]{:S(2)}) %all-to-all-start.17) | async-done | bytes 524320 | tf_op jit(solution)/shard_map/all_to_all | solution.py:201
  682.9 8.2 collective-permute-done.7
  695.6 6.4 all-to-all-start.18
  705.0 14.5 %all-to-all-done.18 = bf16[64,2,2048]{2,1,0:T(2,128)(2,1)} async-done(((bf16[64,2,2048]{2,1,0:T(2,128)(2,1)}), bf16[64,2,2048]{2,1,0:T(2,128)(2,1)}, u32[]{:S(2)}, u32[]{:S(2)}) %all-to-all-start.18) | async-done | bytes 524320 | tf_op jit(solution)/shard_map/all_to_all | solution.py:187
  719.6 15.8 %conditional.19 = (bf16[128,2048]{1,0:T(8,128)(2,1)}) conditional(s32[]{:T(128)} %convert_element_type.473, () %tuple.116, (bf16[64,2,2048]{2,1,0:T(2,128)(2,1)}, bf16[768,2048]{1,0:T(8,128)(2,1)}, f32[2,64,2,1536]{3,2,1,0:T(2,128)}, s32[]{:T(128)}, bf16[2048,1536]{1,0:T(8,128)(2,1)}) %tuple.240), branch_computations={%region_102.103_spmd, %region_103.104_spmd} | conditional | flops 1210286080 | bytes 16252940 | solution.py:198
  726.2 3.4 fusion.50
  729.7 5.7 convolution_convert_fusion.9
  737.6 5.9 all-to-all-start.19
  746.2 14.9 %all-to-all-done.19 = bf16[64,2,2048]{2,1,0:T(2,128)(2,1)} async-done(((bf16[64,2,2048]{2,1,0:T(2,128)(2,1)}), bf16[64,2,2048]{2,1,0:T(2,128)(2,1)}, u32[]{:S(2)}, u32[]{:S(2)}) %all-to-all-start.19) | async-done | bytes 524320 | tf_op jit(solution)/shard_map/all_to_all | solution.py:201
  763.8 24.1 %all_to_all.118 = f32[64,1,2080]{2,1,0:T(1,128)S(1)} all-to-all(f32[64,1,2080]{2,1,0:T(1,128)S(1)} %copy.139), channel_id=1, replica_groups=mesh['section'=4,'expert'=64] {'expert'}, dimensions={0} | all-to-all | bytes 1064960 | tf_op jit(solution)/shard_map/all_to_all | solution.py:229
  789.3 5.7 all-to-all-start.21
  798.1 15.3 %all-to-all-done.21 = f32[64,1,2080]{2,1,0:T(1,128)S(1)} async-done(((f32[64,1,2080]{2,1,0:T(1,128)}), f32[64,1,2080]{2,1,0:T(1,128)S(1)}, u32[]{:S(2)}, u32[]{:S(2)}) %all-to-all-start.21) | async-done | bytes 532512 | tf_op jit(solution)/shard_map/all_to_all | solution.py:231
  (422 shorter events, 216.4 us)
Async XLA Ops:
  0.6 21.9 %copy-start = (bf16[1,2048,64]{1,2,0:T(8,128)(2,1)S(1)}, bf16[1,2048,64]{1,2,0:T(8,128)(2,1)}, u32[]{:S(2)}) copy-start(bf16[1,2048,64]{1,2,0:T(8,128)(2,1)} %param.32) | copy-start | bytes 786436
  0.6 21.9 %copy-start.1 = (bf16[2,64,2048]{2,1,0:T(8,128)(2,1)S(1)}, bf16[2,64,2048]{2,1,0:T(8,128)(2,1)}, u32[]{:S(2)}) copy-start(bf16[2,64,2048]{2,1,0:T(8,128)(2,1)} %param.28) | copy-start | bytes 1572868
  0.7 21.9 %copy-start.10 = (f32[1,2048]{1,0:T(1,128)S(1)}, f32[1,2048]{1,0:T(1,128)}, u32[]{:S(2)}) copy-start(f32[1,2048]{1,0:T(1,128)} %param.31) | copy-start | bytes 24580
  2.2 425.2 %copy-start.25 = (s32[1,1,64,2]{2,3,1,0:T(2,128)}, s32[1,1,64,2]{2,3,1,0:T(2,128)S(1)}, u32[]{:S(2)}) copy-start(s32[1,1,64,2]{2,3,1,0:T(2,128)S(1)} %get-tuple-element.327) | copy-start | bytes 1540
  2.2 476.8 %copy-start.28 = (s32[1,1,64,2]{2,3,1,0:T(2,128)}, s32[1,1,64,2]{2,3,1,0:T(2,128)S(1)}, u32[]{:S(2)}) copy-start(s32[1,1,64,2]{2,3,1,0:T(2,128)S(1)} %get-tuple-element.328) | copy-start | bytes 1540
  9.4 30.8 %all-to-all-start = ((bf16[64,2,2048]{2,1,0:T(2,128)(2,1)}), bf16[64,2,2048]{2,1,0:T(2,128)(2,1)S(1)}, u32[]{:S(2)}, u32[]{:S(2)}) async-start(bf16[64,2,2048]{2,1,0:T(2,128)(2,1)} %reshape.826), calls=%async_computation | async-start | bytes 1048576 | tf_op jit(solution)/shard_map/all_to_all | solution.py:125
  47.1 26.2 %copy-start.11 = (f32[1,64,2,1536]{3,2,1,0:T(2,128)}, f32[1,64,2,1536]{3,2,1,0:T(2,128)S(1)}, u32[]{:S(2)}) copy-start(f32[1,64,2,1536]{3,2,1,0:T(2,128)S(1)} %get-tuple-element.232) | copy-start | bytes 2359300
  48.3 23.4 %all-to-all-start.1 = ((bf16[64,2,2048]{2,1,0:T(2,128)(2,1)}), bf16[64,2,2048]{2,1,0:T(2,128)(2,1)S(1)}, u32[]{:S(2)}, u32[]{:S(2)}) async-start(bf16[64,2,2048]{2,1,0:T(2,128)(2,1)} %reshape.827), calls=%async_computation.1 | async-start | bytes 1048576 | tf_op jit(solution)/shard_map/all_to_all | solution.py:140
  73.3 6.8 collective-permute-start
  80.3 60.7 %copy-start.4 = (bf16[64,2048]{1,0:T(8,128)(2,1)}, bf16[64,2048]{1,0:T(8,128)(2,1)S(1)}, u32[]{:S(2)}) copy-start(bf16[64,2048]{1,0:T(8,128)(2,1)S(1)} %get-tuple-element.316) | copy-start | bytes 786436
  81.8 24.1 %all-to-all-start.2 = ((bf16[64,2,2048]{2,1,0:T(2,128)(2,1)}), bf16[64,2,2048]{2,1,0:T(2,128)(2,1)S(1)}, u32[]{:S(2)}, u32[]{:S(2)}) async-start(bf16[64,2,2048]{2,1,0:T(2,128)(2,1)} %reshape.829), calls=%async_computation.2 | async-start | bytes 1048576 | tf_op jit(solution)/shard_map/all_to_all | solution.py:125
  113.6 27.4 %copy-start.13 = (f32[1,64,2,1536]{3,2,1,0:T(2,128)}, f32[1,64,2,1536]{3,2,1,0:T(2,128)S(1)}, u32[]{:S(2)}) copy-start(f32[1,64,2,1536]{3,2,1,0:T(2,128)S(1)} %get-tuple-element.233) | copy-start | bytes 2359300
  116.1 23.4 %all-to-all-start.3 = ((bf16[64,2,2048]{2,1,0:T(2,128)(2,1)}), bf16[64,2,2048]{2,1,0:T(2,128)(2,1)S(1)}, u32[]{:S(2)}, u32[]{:S(2)}) async-start(bf16[64,2,2048]{2,1,0:T(2,128)(2,1)} %reshape.830), calls=%async_computation.3 | async-start | bytes 1048576 | tf_op jit(solution)/shard_map/all_to_all | solution.py:140
  141.1 18.3 %copy-start.2 = (bf16[2,64,2048]{2,1,0:T(8,128)(2,1)S(1)}, bf16[2,64,2048]{2,1,0:T(8,128)(2,1)}, u32[]{:S(2)}) copy-start(bf16[2,64,2048]{2,1,0:T(8,128)(2,1)} %param.29) | copy-start | bytes 1572868
  141.1 9.5 %collective-permute-start.1 = (bf16[64,2048]{1,0:T(8,128)(2,1)S(1)}, bf16[64,2048]{1,0:T(8,128)(2,1)S(1)}, u32[]{:S(2)}, u32[]{:S(2)}) collective-permute-start(bf16[64,2048]{1,0:T(8,128)(2,1)S(1)} %fusion.166), channel_id=1, source_target_pairs={{0,64},{64,128},{128,192},{1,65},{65,129},{129,193},{2,66},{66,130... | collective-permute-start | bytes 786440 | tf_op jit(solution)/shard_map/ppermute | solution.py:12
  146.3 15.4 %copy-start.12 = (f32[1,64,2,1536]{3,2,1,0:T(2,128)S(1)}, f32[1,64,2,1536]{3,2,1,0:T(2,128)}, u32[]{:S(2)}) copy-start(f32[1,64,2,1536]{3,2,1,0:T(2,128)} %copy-done.11) | copy-start | bytes 2359300
  150.8 12.2 %copy-start.6 = (bf16[64,2048]{1,0:T(8,128)(2,1)}, bf16[64,2048]{1,0:T(8,128)(2,1)S(1)}, u32[]{:S(2)}) copy-start(bf16[64,2048]{1,0:T(8,128)(2,1)S(1)} %get-tuple-element.314) | copy-start | bytes 786436
  152.3 23.9 %all-to-all-start.4 = ((bf16[64,2,2048]{2,1,0:T(2,128)(2,1)}), bf16[64,2,2048]{2,1,0:T(2,128)(2,1)S(1)}, u32[]{:S(2)}, u32[]{:S(2)}) async-start(bf16[64,2,2048]{2,1,0:T(2,128)(2,1)} %reshape.832), calls=%async_computation.4 | async-start | bytes 1048576 | tf_op jit(solution)/shard_map/all_to_all | solution.py:125
  177.6 23.7 %all-to-all-start.5 = ((bf16[64,2,2048]{2,1,0:T(2,128)(2,1)}), bf16[64,2,2048]{2,1,0:T(2,128)(2,1)}, u32[]{:S(2)}, u32[]{:S(2)}) async-start(bf16[64,2,2048]{2,1,0:T(2,128)(2,1)} %reshape.833), calls=%async_computation.5 | async-start | bytes 1048576 | tf_op jit(solution)/shard_map/all_to_all | solution.py:140
  203.3 14.3 %copy-start.5 = (bf16[64,2048]{1,0:T(8,128)(2,1)S(1)}, bf16[64,2048]{1,0:T(8,128)(2,1)}, u32[]{:S(2)}) copy-start(bf16[64,2048]{1,0:T(8,128)(2,1)} %copy-done.4) | copy-start | bytes 786436
  203.3 14.3 %copy-start.17 = (bf16[1,64,2048]{2,1,0:T(8,128)(2,1)S(1)}, bf16[1,64,2048]{2,1,0:T(8,128)(2,1)}, u32[]{:S(2)}) copy-start(bf16[1,64,2048]{2,1,0:T(8,128)(2,1)} %constant_dynamic-slice_fusion.33) | copy-start | bytes 786436
  206.8 16.0 %collective-permute-start.2 = (bf16[64,2048]{1,0:T(8,128)(2,1)S(1)}, bf16[64,2048]{1,0:T(8,128)(2,1)S(1)}, u32[]{:S(2)}, u32[]{:S(2)}) collective-permute-start(bf16[64,2048]{1,0:T(8,128)(2,1)S(1)} %fusion.170), channel_id=1, source_target_pairs={{0,64},{64,128},{128,192},{1,65},{65,129},{129,193},{2,66},{66,130... | collective-permute-start | bytes 786440 | tf_op jit(solution)/shard_map/ppermute | solution.py:12
  227.0 24.0 %all-to-all-start.6 = ((bf16[64,2,2048]{2,1,0:T(2,128)(2,1)}), bf16[64,2,2048]{2,1,0:T(2,128)(2,1)}, u32[]{:S(2)}, u32[]{:S(2)}) async-start(bf16[64,2,2048]{2,1,0:T(2,128)(2,1)} %reshape.835), calls=%async_computation.6 | async-start | bytes 1048576 | tf_op jit(solution)/shard_map/all_to_all | solution.py:125
  255.2 23.5 %all-to-all-start.7 = ((bf16[64,2,2048]{2,1,0:T(2,128)(2,1)}), bf16[64,2,2048]{2,1,0:T(2,128)(2,1)}, u32[]{:S(2)}, u32[]{:S(2)}) async-start(bf16[64,2,2048]{2,1,0:T(2,128)(2,1)} %reshape.836), calls=%async_computation.7 | async-start | bytes 1048576 | tf_op jit(solution)/shard_map/all_to_all | solution.py:140
  284.2 9.4 %collective-permute-start.3 = (bf16[64,2048]{1,0:T(8,128)(2,1)S(1)}, bf16[64,2048]{1,0:T(8,128)(2,1)S(1)}, u32[]{:S(2)}, u32[]{:S(2)}) collective-permute-start(bf16[64,2048]{1,0:T(8,128)(2,1)S(1)} %fusion.174), channel_id=1, source_target_pairs={{0,64},{64,128},{128,192},{1,65},{65,129},{129,193},{2,66},{66,130... | collective-permute-start | bytes 786440 | tf_op jit(solution)/shard_map/ppermute | solution.py:12
  296.0 23.9 %all-to-all-start.9 = ((bf16[64,2,2048]{2,1,0:T(2,128)(2,1)}), bf16[64,2,2048]{2,1,0:T(2,128)(2,1)S(1)}, u32[]{:S(2)}, u32[]{:S(2)}) async-start(bf16[64,2,2048]{2,1,0:T(2,128)(2,1)} %reshape.839), calls=%async_computation.9 | async-start | bytes 1048576 | tf_op jit(solution)/shard_map/all_to_all | solution.py:125
  303.4 92.8 %copy-start.45 = (f32[64]{0:T(128)}, f32[64]{0:T(128)S(1)}, u32[]{:S(2)}) copy-start(f32[64]{0:T(128)S(1)} %add_rsqrt_fusion.5) | copy-start | bytes 772
  319.9 23.7 %all-to-all-start.8 = ((bf16[64,2,2048]{2,1,0:T(2,128)(2,1)}), bf16[64,2,2048]{2,1,0:T(2,128)(2,1)}, u32[]{:S(2)}, u32[]{:S(2)}) async-start(bf16[64,2,2048]{2,1,0:T(2,128)(2,1)} %reshape.838), calls=%async_computation.8 | async-start | bytes 1048576 | tf_op jit(solution)/shard_map/all_to_all | solution.py:187
  343.6 23.4 %all-to-all-start.11 = ((bf16[64,2,2048]{2,1,0:T(2,128)(2,1)}), bf16[64,2,2048]{2,1,0:T(2,128)(2,1)S(1)}, u32[]{:S(2)}, u32[]{:S(2)}) async-start(bf16[64,2,2048]{2,1,0:T(2,128)(2,1)} %reshape.842), calls=%async_computation.11 | async-start | bytes 1048576 | tf_op jit(solution)/shard_map/all_to_all | solution.py:140
  366.9 23.9 %all-to-all-start.10 = ((bf16[64,2,2048]{2,1,0:T(2,128)(2,1)}), bf16[64,2,2048]{2,1,0:T(2,128)(2,1)}, u32[]{:S(2)}, u32[]{:S(2)}) async-start(bf16[64,2,2048]{2,1,0:T(2,128)(2,1)} %reshape.840), calls=%async_computation.10 | async-start | bytes 1048576 | tf_op jit(solution)/shard_map/all_to_all | solution.py:201
  377.2 19.0 %copy-start.3 = (bf16[2,64,2048]{2,1,0:T(8,128)(2,1)S(1)}, bf16[2,64,2048]{2,1,0:T(8,128)(2,1)}, u32[]{:S(2)}) copy-start(bf16[2,64,2048]{2,1,0:T(8,128)(2,1)} %param.29) | copy-start | bytes 1572868
  378.6 18.6 %copy-start.22 = (bf16[64,64]{1,0:T(8,128)(2,1)}, bf16[64,64]{1,0:T(8,128)(2,1)S(1)}, u32[]{:S(2)}) copy-start(bf16[64,64]{1,0:T(8,128)(2,1)S(1)} %select_reduce_fusion.16) | copy-start | bytes 24580
  397.2 19.5 %collective-permute-start.4 = (bf16[64,2048]{1,0:T(8,128)(2,1)}, bf16[64,2048]{1,0:T(8,128)(2,1)}, u32[]{:S(2)}, u32[]{:S(2)}) collective-permute-start(bf16[64,2048]{1,0:T(8,128)(2,1)} %get-tuple-element.306), channel_id=1, source_target_pairs={{64,0},{128,64},{192,128},{65,1},{129,65},{193,129},{66,2},{130,66... | collective-permute-start | bytes 786440 | tf_op jit(solution)/shard_map/ppermute | solution.py:12
  398.5 77.2 %copy-start.34 = (f32[64]{0:T(128)}, f32[64]{0:T(128)S(1)}, u32[]{:S(2)}) copy-start(f32[64]{0:T(128)S(1)} %add_rsqrt_fusion.3) | copy-start | bytes 772
  421.1 23.7 %all-to-all-start.12 = ((bf16[64,2,2048]{2,1,0:T(2,128)(2,1)}), bf16[64,2,2048]{2,1,0:T(2,128)(2,1)}, u32[]{:S(2)}, u32[]{:S(2)}) async-start(bf16[64,2,2048]{2,1,0:T(2,128)(2,1)} %reshape.844), calls=%async_computation.12 | async-start | bytes 1048576 | tf_op jit(solution)/shard_map/all_to_all | solution.py:187
  427.5 62.0 %copy-start.30 = (s32[2,64]{1,0:T(2,128)}, s32[2,64]{1,0:T(2,128)S(1)}, u32[]{:S(2)}) copy-start(s32[2,64]{1,0:T(2,128)S(1)} %copy.133) | copy-start | bytes 1540
  447.9 23.5 %all-to-all-start.13 = ((bf16[64,2,2048]{2,1,0:T(2,128)(2,1)}), bf16[64,2,2048]{2,1,0:T(2,128)(2,1)}, u32[]{:S(2)}, u32[]{:S(2)}) async-start(bf16[64,2,2048]{2,1,0:T(2,128)(2,1)} %reshape.845), calls=%async_computation.13 | async-start | bytes 1048576 | tf_op jit(solution)/shard_map/all_to_all | solution.py:201
  453.8 23.9 %copy-start.35 = (f32[64]{0:T(128)}, f32[64]{0:T(128)S(1)}, u32[]{:S(2)}) copy-start(f32[64]{0:T(128)S(1)} %add_rsqrt_fusion.2) | copy-start | bytes 772
  454.4 35.1 %copy-start.20 = (bf16[64,64]{1,0:T(8,128)(2,1)}, bf16[64,64]{1,0:T(8,128)(2,1)S(1)}, u32[]{:S(2)}) copy-start(bf16[64,64]{1,0:T(8,128)(2,1)S(1)} %select_reduce_fusion.12) | copy-start | bytes 24580
  475.7 23.6 %copy-start.42 = (s32[128]{0:T(128)S(1)}, s32[128]{0:T(128)}, u32[]{:S(2)}) copy-start(s32[128]{0:T(128)} %eq.414) | copy-start | bytes 1540
  477.7 10.7 %collective-permute-start.5 = (bf16[64,2048]{1,0:T(8,128)(2,1)}, bf16[64,2048]{1,0:T(8,128)(2,1)}, u32[]{:S(2)}, u32[]{:S(2)}) collective-permute-start(bf16[64,2048]{1,0:T(8,128)(2,1)} %get-tuple-element.302), channel_id=1, source_target_pairs={{64,0},{128,64},{192,128},{65,1},{129,65},{193,129},{66,2},{130,66... | collective-permute-start | bytes 786440 | tf_op jit(solution)/shard_map/ppermute | solution.py:12
  479.2 20.2 %copy-start.32 = (f32[64,2]{0,1:T(2,128)}, f32[64,2]{0,1:T(2,128)S(1)}, u32[]{:S(2)}) copy-start(f32[64,2]{0,1:T(2,128)S(1)} %add_divide_fusion.7) | copy-start | bytes 1540
  492.9 23.9 %all-to-all-start.14 = ((bf16[64,2,2048]{2,1,0:T(2,128)(2,1)}), bf16[64,2,2048]{2,1,0:T(2,128)(2,1)}, u32[]{:S(2)}, u32[]{:S(2)}) async-start(bf16[64,2,2048]{2,1,0:T(2,128)(2,1)} %reshape.847), calls=%async_computation.14 | async-start | bytes 1048576 | tf_op jit(solution)/shard_map/all_to_all | solution.py:187
  507.1 172.3 %copy-start.38 = (f32[64]{0:T(128)}, f32[64]{0:T(128)S(1)}, u32[]{:S(2)}) copy-start(f32[64]{0:T(128)S(1)} %add_rsqrt_fusion.1) | copy-start | bytes 772
  517.6 10.4 %copy-start.29 = (s32[1,1,64,2]{2,3,1,0:T(2,128)S(1)}, s32[1,1,64,2]{2,3,1,0:T(2,128)}, u32[]{:S(2)}) copy-start(s32[1,1,64,2]{2,3,1,0:T(2,128)} %copy-done.28) | copy-start | bytes 1540
  517.6 27.9 %copy-start.31 = (s32[2,64]{1,0:T(2,128)S(1)}, s32[2,64]{1,0:T(2,128)}, u32[]{:S(2)}) copy-start(s32[2,64]{1,0:T(2,128)} %copy-done.30) | copy-start | bytes 1540
  519.8 27.1 %copy-start.36 = (f32[64]{0:T(128)S(1)}, f32[64]{0:T(128)}, u32[]{:S(2)}) copy-start(f32[64]{0:T(128)} %copy-done.35) | copy-start | bytes 772
  519.8 23.6 %all-to-all-start.15 = ((bf16[64,2,2048]{2,1,0:T(2,128)(2,1)}), bf16[64,2,2048]{2,1,0:T(2,128)(2,1)}, u32[]{:S(2)}, u32[]{:S(2)}) async-start(bf16[64,2,2048]{2,1,0:T(2,128)(2,1)} %reshape.848), calls=%async_computation.15 | async-start | bytes 1048576 | tf_op jit(solution)/shard_map/all_to_all | solution.py:201
  528.0 22.6 %copy-start.27 = (s32[1,1,64,2]{2,3,1,0:T(2,128)S(1)}, s32[1,1,64,2]{2,3,1,0:T(2,128)}, u32[]{:S(2)}) copy-start(s32[1,1,64,2]{2,3,1,0:T(2,128)} %get-tuple-element.336) | copy-start | bytes 1540
  547.3 69.4 %copy-start.46 = (f32[64]{0:T(128)S(1)}, f32[64]{0:T(128)}, u32[]{:S(2)}) copy-start(f32[64]{0:T(128)} %get-tuple-element.257) | copy-start | bytes 772
  549.3 56.6 %collective-permute-start.6 = (bf16[64,2048]{1,0:T(8,128)(2,1)}, bf16[64,2048]{1,0:T(8,128)(2,1)}, u32[]{:S(2)}, u32[]{:S(2)}) collective-permute-start(bf16[64,2048]{1,0:T(8,128)(2,1)} %get-tuple-element.298), channel_id=1, source_target_pairs={{64,0},{128,64},{192,128},{65,1},{129,65},{193,129},{66,2},{130,66... | collective-permute-start | bytes 786440 | tf_op jit(solution)/shard_map/ppermute | solution.py:12
  610.3 23.7 %all-to-all-start.16 = ((bf16[64,2,2048]{2,1,0:T(2,128)(2,1)}), bf16[64,2,2048]{2,1,0:T(2,128)(2,1)}, u32[]{:S(2)}, u32[]{:S(2)}) async-start(bf16[64,2,2048]{2,1,0:T(2,128)(2,1)} %reshape.850), calls=%async_computation.16 | async-start | bytes 1048576 | tf_op jit(solution)/shard_map/all_to_all | solution.py:187
  616.7 41.3 %copy-start.40 = (f32[64]{0:T(128)}, f32[64]{0:T(128)S(1)}, u32[]{:S(2)}) copy-start(f32[64]{0:T(128)S(1)} %add_rsqrt_fusion) | copy-start | bytes 772
  652.1 23.5 %all-to-all-start.17 = ((bf16[64,2,2048]{2,1,0:T(2,128)(2,1)}), bf16[64,2,2048]{2,1,0:T(2,128)(2,1)}, u32[]{:S(2)}, u32[]{:S(2)}) async-start(bf16[64,2,2048]{2,1,0:T(2,128)(2,1)} %reshape.851), calls=%async_computation.17 | async-start | bytes 1048576 | tf_op jit(solution)/shard_map/all_to_all | solution.py:201
  660.1 22.6 %copy-start.26 = (s32[1,1,64,2]{2,3,1,0:T(2,128)S(1)}, s32[1,1,64,2]{2,3,1,0:T(2,128)}, u32[]{:S(2)}) copy-start(s32[1,1,64,2]{2,3,1,0:T(2,128)} %copy-done.25) | copy-start | bytes 1540
  679.4 22.5 %copy-start.23 = (bf16[64,64]{1,0:T(8,128)(2,1)S(1)}, bf16[64,64]{1,0:T(8,128)(2,1)}, u32[]{:S(2)}) copy-start(bf16[64,64]{1,0:T(8,128)(2,1)} %copy-done.22) | copy-start | bytes 24580
  679.4 23.5 %copy-start.21 = (bf16[64,64]{1,0:T(8,128)(2,1)S(1)}, bf16[64,64]{1,0:T(8,128)(2,1)}, u32[]{:S(2)}) copy-start(bf16[64,64]{1,0:T(8,128)(2,1)} %copy-done.20) | copy-start | bytes 24580
  681.4 9.7 %collective-permute-start.7 = (bf16[64,2048]{1,0:T(8,128)(2,1)}, bf16[64,2048]{1,0:T(8,128)(2,1)}, u32[]{:S(2)}, u32[]{:S(2)}) collective-permute-start(bf16[64,2048]{1,0:T(8,128)(2,1)} %get-tuple-element.294), channel_id=1, source_target_pairs={{64,0},{128,64},{192,128},{65,1},{129,65},{193,129},{66,2},{130,66... | collective-permute-start | bytes 786440 | tf_op jit(solution)/shard_map/ppermute | solution.py:12
  682.9 21.0 %copy-start.37 = (f32[64]{0:T(128)S(1)}, f32[64]{0:T(128)}, u32[]{:S(2)}) copy-start(f32[64]{0:T(128)} %copy-done.35) | copy-start | bytes 772
  695.6 24.0 %all-to-all-start.18 = ((bf16[64,2,2048]{2,1,0:T(2,128)(2,1)}), bf16[64,2,2048]{2,1,0:T(2,128)(2,1)}, u32[]{:S(2)}, u32[]{:S(2)}) async-start(bf16[64,2,2048]{2,1,0:T(2,128)(2,1)} %reshape.853), calls=%async_computation.18 | async-start | bytes 1048576 | tf_op jit(solution)/shard_map/all_to_all | solution.py:187
  719.6 23.9 %copy-start.39 = (f32[64]{0:T(128)S(1)}, f32[64]{0:T(128)}, u32[]{:S(2)}) copy-start(f32[64]{0:T(128)} %copy-done.38) | copy-start | bytes 772
  737.6 23.5 %all-to-all-start.19 = ((bf16[64,2,2048]{2,1,0:T(2,128)(2,1)}), bf16[64,2,2048]{2,1,0:T(2,128)(2,1)}, u32[]{:S(2)}, u32[]{:S(2)}) async-start(bf16[64,2,2048]{2,1,0:T(2,128)(2,1)} %reshape.854), calls=%async_computation.19 | async-start | bytes 1048576 | tf_op jit(solution)/shard_map/all_to_all | solution.py:201
  745.5 17.6 %copy-start.24 = (f32[2048]{0:T(1024)S(1)}, f32[2048]{0:T(1024)}, u32[]{:S(2)}) copy-start(f32[2048]{0:T(1024)} %get-tuple-element.249) | copy-start | bytes 24580
  789.3 24.1 %all-to-all-start.21 = ((f32[64,1,2080]{2,1,0:T(1,128)}), f32[64,1,2080]{2,1,0:T(1,128)S(1)}, u32[]{:S(2)}, u32[]{:S(2)}) async-start(f32[64,1,2080]{2,1,0:T(1,128)} %broadcast_in_dim.304), calls=%async_computation.21 | async-start | bytes 1114112 | tf_op jit(solution)/shard_map/all_to_all | solution.py:231
  (11 other events, 48.7 us)

commit v2 on v0

v2 whole, which is shorter than its diff:
```python
import functools

import jax
import jax.numpy as jnp
from jax import lax
from jax.experimental import pallas as pl
from jax.experimental.pallas import tpu as pltpu
from jax.sharding import PartitionSpec as P

EPSILON = 1e-06
CHUNKS = 2
MESH = pl.DeviceIdType.MESH
F32 = jnp.float32
BF16 = jnp.bfloat16


def dot_nn(left, right):
    return jnp.dot(left, right, preferred_element_type=F32)


def dot_nt(left, right):
    return lax.dot_general(left, right, (((1,), (1,)), ((), ())), preferred_element_type=F32)


def dot_tn(left, right):
    return lax.dot_general(left, right, (((0,), (0,)), ((), ())), preferred_element_type=F32)


def wait_bytes(ref, sem):
    pltpu.make_async_copy(ref, ref, sem).wait()


def peer_of(me, step, experts):
    if experts != 64:
        return lax.rem(me + step + 1, experts)
    far, near = step // 8, lax.rem(step + 1, 8)
    half = (far + 1) // 2
    shift_z = 4 + half * (1 - 2 * lax.rem(far, 2))
    my_z, my_y, my_core = me // 8, lax.rem(me // 2, 4), lax.rem(me, 2)
    to_z = lax.rem(my_z + shift_z, 8)
    to_y = lax.rem(my_y + near // 2, 4)
    to_core = lax.rem(my_core + lax.rem(near, 2), 2)
    return (to_z * 4 + to_y) * 2 + to_core


def kernel(
    experts, sections, denominator,
    inputs, cotangent, lengths, gain, router, w_in_hbm, w_out_hbm, routes,
    grads_out, router_out, gain_out,
    w_in, w_out, h_in, h_out, d_in, d_out,
    x_send, x_recv, y_send, y_recv, g_send, g_recv, r_send, r_recv, p_send, p_recv,
    f_send, f_recv, mixed, joined, q_keep, take, give, stats, logit_keep, column, gain_part,
    weight_sem, out_sem, h_sem, d_sem, x_sem, y_sem, g_sem, r_sem, p_sem, f_sem,
    xs_sem, ys_sem, gs_sem, rs_sem, ps_sem, fs_sem, hs_sem, ds_sem,
):
    section = lax.axis_index("section")
    me = lax.axis_index("expert")
    micros, tokens, width = inputs.shape
    hidden = w_out.shape[0]
    slots = 2 * experts
    piece = width // CHUNKS
    chunk_ids = range(CHUNKS)

    def cols(index):
        return pl.ds(index * piece, piece)

    load_in = pltpu.make_async_copy(w_in_hbm.at[0, 0], w_in, weight_sem.at[0])
    load_out = pltpu.make_async_copy(w_out_hbm.at[0, 0], w_out, weight_sem.at[1])

    @pl.when(section == 0)
    def _():
        for m in range(micros):
            for c in chunk_ids:
                pltpu.make_async_copy(inputs.at[m, :, cols(c)], h_in.at[m, c], h_sem.at[m, c]).start()

    load_in.start()
    load_out.start()

    @pl.when(section == sections - 1)
    def _():
        for m in range(micros):
            for c in chunk_ids:
                pltpu.make_async_copy(cotangent.at[m, :, cols(c)], d_in.at[m, c], d_sem.at[m, c]).start()

    barrier = pltpu.get_barrier_semaphore()

    def greet(step, carry):
        pl.semaphore_signal(barrier, inc=1, device_id={"expert": peer_of(me, step, experts)}, device_id_type=MESH)
        return carry

    lax.fori_loop(0, experts - 1, greet, 0)

    @pl.when(section > 0)
    def _():
        pl.semaphore_signal(barrier, inc=1, device_id={"section": section - 1}, device_id_type=MESH)

    @pl.when(section < sections - 1)
    def _():
        pl.semaphore_signal(barrier, inc=1, device_id={"section": section + 1}, device_id_type=MESH)

    column[...] = jnp.zeros_like(column)
    gain_part[...] = jnp.zeros_like(gain_part)
    expert_codes = lax.broadcasted_iota(jnp.int32, (tokens, experts), 1)

    def chosen_of(m, k):
        return routes[0, m][:, k : k + 1] == expert_codes

    earlier = (
        lax.broadcasted_iota(jnp.int32, (tokens, tokens), 1)
        < lax.broadcasted_iota(jnp.int32, (tokens, tokens), 0)
    ).astype(F32).astype(BF16)
    slot_codes = lax.broadcasted_iota(jnp.int32, (tokens, slots), 1).astype(F32)
    positions = lax.broadcasted_iota(jnp.int32, (tokens, 1), 0)
    for m in range(micros):
        live = positions < lengths[m : m + 1, :]
        tables = []
        for k in range(2):
            marked = chosen_of(m, k).astype(F32)
            rank = jnp.sum(marked * dot_nn(earlier, marked.astype(BF16)), axis=1, keepdims=True)
            slot = routes[0, m][:, k : k + 1].astype(F32) * 2.0 + rank
            tables.append(((slot == slot_codes) & live).astype(F32))
        table = jnp.concatenate(tables, axis=0)
        give[m] = table.astype(BF16)
        take[m] = table.T.astype(BF16)

    pl.semaphore_wait(
        barrier,
        experts - 1 + (section > 0).astype(jnp.int32) + (section < sections - 1).astype(jnp.int32),
    )

    def scatter(source, target, send_sem, recv_sem):
        pltpu.make_async_copy(source(me), target, recv_sem).start()

        def one(step, carry):
            peer = peer_of(me, step, experts)
            pltpu.make_async_remote_copy(
                src_ref=source(peer), dst_ref=target, send_sem=send_sem, recv_sem=recv_sem,
                device_id={"expert": peer}, device_id_type=MESH,
            ).start()
            return carry

        lax.fori_loop(0, experts - 1, one, 0)

    def exchange(m, c, values, sends, receives, send_sem, recv_sem):
        sends[m, :, :, cols(c)] = values.astype(BF16).reshape(experts, 2, piece)
        scatter(
            lambda peer: sends.at[m, peer, :, cols(c)], receives.at[m, me, :, cols(c)],
            send_sem.at[m, c], recv_sem.at[m, c],
        )

    def rows_of(buffer, m, c):
        return buffer[m, :, :, cols(c)].reshape(slots, piece)

    def values_of(m, c):
        return h_in[m, c].astype(F32)

    def gain_of(c):
        return gain[:, c * piece : (c + 1) * piece]

    def forward(m, carry):
        square = jnp.zeros((tokens, 1), F32)
        for c in chunk_ids:
            wait_bytes(h_in.at[m, c], h_sem.at[m, c])
            values = values_of(m, c)
            square += jnp.sum(values * values, axis=1, keepdims=True)
        scale = lax.rsqrt(square / width + EPSILON)
        logits = jnp.zeros((tokens, experts), F32)
        for c in chunk_ids:
            normed = (values_of(m, c) * scale * gain_of(c)).astype(BF16)
            exchange(m, c, dot_nn(take[m], jnp.concatenate([normed, normed], axis=0)), x_send, x_recv, xs_sem, x_sem)
            logits += dot_nn(normed, router[0, c * piece : (c + 1) * piece, :])
        picked = [
            jnp.sum(jnp.where(chosen_of(m, k), logits, 0.0), axis=1, keepdims=True) for k in range(2)
        ]
        first, second = jax.nn.sigmoid(picked[0] - picked[1]), jax.nn.sigmoid(picked[1] - picked[0])
        for index, stat in enumerate((scale, first, second)):
            stats[m, index] = jnp.broadcast_to(stat, (tokens, 128))

        @pl.when(m == 0)
        def _():
            load_in.wait()
            load_out.wait()

        for c in chunk_ids:
            wait_bytes(x_recv.at[m, :, :, cols(c)], x_sem.at[m, c])
            part = dot_nn(rows_of(x_recv, m, c), w_in[c * piece : (c + 1) * piece, :])
            mixed[m] = part if c == 0 else mixed[m] + part
        gate, up = mixed[m, :, :hidden], mixed[m, :, hidden:]
        activated = (gate * jax.nn.sigmoid(gate) * up).astype(BF16)
        for c in chunk_ids:
            exchange(m, c, dot_nn(activated, w_out[:, c * piece : (c + 1) * piece]), y_send, y_recv, ys_sem, y_sem)
        for c in chunk_ids:
            wait_bytes(y_recv.at[m, :, :, cols(c)], y_sem.at[m, c])
            per_choice = dot_nn(give[m], rows_of(y_recv, m, c))
            combined = first * per_choice[:tokens] + second * per_choice[tokens:]
            h_out[m, c] = (values_of(m, c) + combined).astype(BF16)

            @pl.when(section < sections - 1)
            def _():
                pltpu.make_async_remote_copy(
                    src_ref=h_out.at[m, c], dst_ref=h_in.at[m, c], send_sem=hs_sem.at[m, c],
                    recv_sem=h_sem.at[m, c], device_id={"section": section + 1}, device_id_type=MESH,
                ).start()

        return carry

    lax.fori_loop(0, micros, forward, 0)

    def backward(m, carry):
        scale, first, second = (stats[m, index][:, :1] for index in range(3))
        for c in chunk_ids:
            wait_bytes(d_in.at[m, c], d_sem.at[m, c])
            grad = d_in[m, c].astype(F32)
            pair = jnp.concatenate([(first * grad).astype(BF16), (second * grad).astype(BF16)], axis=0)
            exchange(m, c, dot_nn(take[m], pair), g_send, g_recv, gs_sem, g_sem)
        difference = jnp.zeros((tokens, 1), F32)
        for c in chunk_ids:
            per_choice = dot_nn(give[m], rows_of(y_recv, m, c))
            grad = d_in[m, c].astype(F32)
            difference += jnp.sum(grad * per_choice[:tokens], axis=1, keepdims=True) - jnp.sum(
                grad * per_choice[tokens:], axis=1, keepdims=True
            )
        pick = first * second * difference
        picks = jnp.concatenate([pick, -pick], axis=0)
        lanes = lax.broadcasted_iota(jnp.int32, (2 * tokens, 128), 1)
        picks = jnp.where(lanes == 0, picks, 0.0).astype(BF16)
        p_send[m] = dot_nn(take[m], picks).astype(BF16).reshape(experts, 2, 128)
        scatter(lambda peer: p_send.at[m, peer], p_recv.at[m, me], ps_sem.at[m], p_sem.at[m])
        logit_grad = jnp.where(chosen_of(m, 0), pick, 0.0) + jnp.where(chosen_of(m, 1), -pick, 0.0)
        logit_keep[...] = logit_grad.astype(BF16)

        for c in chunk_ids:
            wait_bytes(g_recv.at[m, :, :, cols(c)], g_sem.at[m, c])
            part = dot_nt(rows_of(g_recv, m, c), w_out[:, c * piece : (c + 1) * piece])
            act_grad = part if c == 0 else act_grad + part
        gate, up = mixed[m, :, :hidden], mixed[m, :, hidden:]
        sigmoid_gate = jax.nn.sigmoid(gate)
        joined[:, :hidden] = (act_grad * up * sigmoid_gate * (1.0 + gate * (1.0 - sigmoid_gate))).astype(BF16)
        joined[:, hidden:] = (act_grad * gate * sigmoid_gate).astype(BF16)
        for c in chunk_ids:
            exchange(m, c, dot_nt(joined[...], w_in[c * piece : (c + 1) * piece, :]), r_send, r_recv, rs_sem, r_sem)
        wait_bytes(p_recv.at[m], p_sem.at[m])
        pick_rows = p_recv[m].reshape(slots, 128)
        for c in chunk_ids:
            rows = rows_of(x_recv, m, c)
            column[:, cols(c)] += dot_tn(pick_rows, rows)[:1]
            row_grads = rows_of(r_send, m, c).astype(F32)
            gain_part[:, cols(c)] += jnp.sum(row_grads * rows.astype(F32), axis=0, keepdims=True)

        @pl.when(m == micros - 1)
        def _():
            mine = (lax.broadcasted_iota(jnp.int32, (8, experts), 1) == me).astype(F32).astype(BF16)
            own_router = dot_nt(mine, router[0])[:1]
            f_send[0] = jnp.concatenate(
                [column[...], (gain_part[...] + own_router * column[...]) / gain[...]], axis=0
            )
            scatter(lambda peer: f_send.at[0], f_recv.at[me], fs_sem, f_sem)

        both = give[m, :tokens] + give[m, tokens:]
        inner = jnp.zeros((tokens, 1), F32)
        for c in chunk_ids:
            base = dot_nt(logit_keep[...], router[0, c * piece : (c + 1) * piece, :])
            wait_bytes(r_recv.at[m, :, :, cols(c)], r_sem.at[m, c])
            scaled = (dot_nn(both, rows_of(r_recv, m, c)) + base) * gain_of(c)
            q_keep[:, cols(c)] = scaled
            inner += jnp.sum(scaled * (values_of(m, c) * scale), axis=1, keepdims=True)
        inner = inner / width
        for c in chunk_ids:
            centred = values_of(m, c) * scale
            grad = d_in[m, c].astype(F32)
            d_out[m, c] = (grad + scale * (q_keep[:, cols(c)] - centred * inner)).astype(BF16)

            @pl.when(section > 0)
            def _():
                pltpu.make_async_remote_copy(
                    src_ref=d_out.at[m, c], dst_ref=d_in.at[m, c], send_sem=ds_sem.at[m, c],
                    recv_sem=d_sem.at[m, c], device_id={"section": section - 1}, device_id_type=MESH,
                ).start()

            pltpu.make_async_copy(d_out.at[m, c], grads_out.at[0, m, :, cols(c)], out_sem.at[m, c]).start()
        return carry

    lax.fori_loop(0, micros, backward, 0)

    wait_bytes(f_recv, f_sem)
    router_out[...] = f_recv[:, 0, :] / denominator
    gain_out[...] = jnp.sum(f_recv[:, 1, :], axis=0, keepdims=True) / denominator

    others = pl.ds(0, experts - 1)

    def drain(m, carry):
        for c in chunk_ids:
            for buffer, sem in ((x_send, xs_sem), (y_send, ys_sem), (g_send, gs_sem), (r_send, rs_sem)):
                wait_bytes(buffer.at[m, others, :, cols(c)], sem.at[m, c])
            wait_bytes(d_out.at[m, c], out_sem.at[m, c])

            @pl.when(section < sections - 1)
            def _():
                wait_bytes(h_out.at[m, c], hs_sem.at[m, c])

            @pl.when(section > 0)
            def _():
                wait_bytes(d_out.at[m, c], ds_sem.at[m, c])

        wait_bytes(p_send.at[m, others], ps_sem.at[m])
        return carry

    lax.fori_loop(0, micros, drain, 0)
    wait_bytes(f_recv.at[others], fs_sem)


def solution(mesh):
    sections, experts = mesh.shape["section"], mesh.shape["expert"]

    def local(inputs, cotangent, lengths, norm_gain, router, expert_in, expert_out, routes):
        micros, tokens, width = inputs.shape
        hidden = expert_out.shape[2]
        piece = width // CHUNKS
        vmem = pl.BlockSpec(memory_space=pltpu.VMEM)
        hbm = pl.BlockSpec(memory_space=pl.ANY)
        DMA = pltpu.SemaphoreType.DMA
        plane = pltpu.VMEM((micros, CHUNKS, tokens, piece), BF16)
        slab = pltpu.VMEM((micros, experts, 2, width), BF16)
        small = pltpu.VMEM((micros, experts, 2, 128), BF16)
        each = DMA((micros, CHUNKS))
        grads, router_rows, gain_row = pl.pallas_call(
            functools.partial(kernel, experts, sections, float(micros * 2 * tokens)),
            out_shape=(
                jax.ShapeDtypeStruct((1, micros, tokens, width), BF16),
                jax.ShapeDtypeStruct((experts, width), F32),
                jax.ShapeDtypeStruct((1, width), F32),
            ),
            in_specs=[hbm, hbm, vmem, vmem, vmem, hbm, hbm, vmem],
            out_specs=(hbm, vmem, vmem),
            scratch_shapes=[
                pltpu.VMEM((width, 2 * hidden), BF16),
                pltpu.VMEM((hidden, width), BF16),
                plane, plane, plane, plane,
                slab, slab, slab, slab, slab, slab, slab, slab, small, small,
                pltpu.VMEM((1, 2, width), F32),
                pltpu.VMEM((experts, 2, width), F32),
                pltpu.VMEM((micros, 2 * experts, 2 * hidden), F32),
                pltpu.VMEM((2 * experts, 2 * hidden), BF16),
                pltpu.VMEM((tokens, width), F32),
                pltpu.VMEM((micros, 2 * experts, 2 * tokens), BF16),
                pltpu.VMEM((micros, 2 * tokens, 2 * experts), BF16),
                pltpu.VMEM((micros, 3, tokens, 128), F32),
                pltpu.VMEM((tokens, experts), BF16),
                pltpu.VMEM((1, width), F32),
                pltpu.VMEM((1, width), F32),
                DMA((2,)), each, each, each, each, each, each, each, DMA((micros,)), DMA,
                each, each, each, each, DMA((micros,)), DMA, each, each,
            ],
            compiler_params=pltpu.CompilerParams(
                collective_id=0, has_side_effects=True, vmem_limit_bytes=60 * 1024 * 1024
            ),
        )(inputs, cotangent, lengths, norm_gain, router, expert_in, expert_out, routes)
        return grads, router_rows.T[None], gain_row

    in_specs = (
        P(None, "expert", None),
        P(None, "expert", None),
        P(None, "expert"),
        P("section", None),
        P("section", None, None),
        P("section", "expert", None, None),
        P("section", "expert", None, None),
        P("section", None, "expert", None),
    )
    out_specs = (P("section", None, "expert", None), P("section", None, None), P("section", None))
    return jax.shard_map(local, mesh=mesh, in_specs=in_specs, out_specs=out_specs, check_vma=False)
```

time: 1080 us -> 406 us (0.38); the launches traced: 1070 us -> 406 us
  waiting for transfers between devices: 551 us -> 0 us
  Pallas kernels: 0 us -> 395 us
  starting transfers between devices: 154 us -> 0 us
  blocking collectives: 128 us -> 0 us
  local copies, waits for them, and re-layouts: 98.3 us -> 9.71 us
  matrix products: 68 us -> 0 us
  other arithmetic: 52.6 us -> 0 us
  between operations: 15.8 us -> 0.64 us
    pallas_call x0 -> x1, Pallas kernels: none -> 395 us  [local(): pl.pallas_call(functools.partial(kernel, experts, sections, float(micros...]
    all_to_all x20 -> x0, waiting for transfers between devices: 262 us -> none  [the longest x5 69.7 us: local(): lax.all_to_all(run_result.reshape(row_shape), 'expert', split_axis=0, con...]
    psum x1 -> x0, waiting for transfers between devices: 182 us -> none  [local(): router_sum, gain_sum = lax.psum((router_total, gain_total), 'expert')]
    all_to_all x20 -> x0, starting transfers between devices: 128 us -> none  [the longest x5 38.4 us: local(): lax.all_to_all(outgoing, 'expert', split_axis=0, concat_axis=0, tiled=True)]
    psum x1 -> x0, blocking collectives: 128 us -> none  [local(): router_sum, gain_sum = lax.psum((router_total, gain_total), 'expert')]
    ppermute x8 -> x0, waiting for transfers between devices: 107 us -> none  [shifted(): return lax.ppermute(block, axis, route)]
    dot_general x47 -> x0, matrix products: 68 us -> none  [the longest x2 10.7 us: expert_adjoint(): lax.dot_general(joined, weight_in, (((1,), (1,)), ((), ())), preferred_el...]
    reshape x41 -> x0, local copies, waits for them, and re-layouts: 60.5 us -> none  [the longest x5 10.9 us: local(): grad_send.astype(jnp.bfloat16).reshape(experts, capacity, model_width)]
  transfers between devices with their start and end apart: 29 -> 0, of which waited for: 28 -> 0; matrix products, arithmetic and copies ran while one was open for 8% -> 0% of each run, Pallas kernels for 0% -> 0%
where the time goes in v2:
time: 406 us
  Pallas kernels  395 us (97%)
  local copies, waits for them, and re-layouts  9.71 us (2%)
    pallas_call x1, Pallas kernels, local(): pl.pallas_call(functools.partial(kernel, experts, sections, float(micros...  395 us
    unnamed x6, local copies, waits for them, and re-layouts  9.71 us

profile of v2, /device:TPU:1, one launch (start us, length us, event | category | flops | bytes accessed | tf_op | source)
XLA Modules:
  0.0 405.5 jit_solution(4873086390596122310)
XLA Ops:
  0.6 1.3 copy.11.lengths
  1.9 1.4 copy.13.routes
  3.3 2.0 copy.12.router
  5.3 395.1 %shard_map.103 = (bf16[1,2,64,2048]{3,2,1,0:T(8,128)(2,1)}, f32[64,2048]{1,0:T(8,128)}, f32[1,2048]{1,0:T(1,128)}) custom-call(bf16[2,64,2048]{2,1,0:T(8,128)(2,1)} %inputs.1, bf16[2,64,2048]{2,1,0:T(8,128)(2,1)} %cotangent.1, s32[2,1]{1,0:T(2,128)} %copy.11.lengths, f32[1,2048]{1,0:T(1,128)} %gain.1, bf16[1,2048,64]{2,1,0:T(8,128)(2,1)} %copy.12.router, ...), custom_call_target="tpu_custom_call" | custom-call | tf_op jit(solution)/shard_map/pallas_call | solution.py:326
  400.5 1.9 copy.17
  402.3 1.9 copy.18
  404.2 1.3 copy.19

commit v3 on v2

v3 whole, which is shorter than its diff:
```python
import functools

import jax
import jax.numpy as jnp
from jax import lax
from jax.experimental import pallas as pl
from jax.experimental.pallas import tpu as pltpu
from jax.sharding import PartitionSpec as P

EPSILON = 1e-06
MESH = pl.DeviceIdType.MESH
F32 = jnp.float32
BF16 = jnp.bfloat16


def dot_nn(left, right):
    return jnp.dot(left, right, preferred_element_type=F32)


def dot_nt(left, right):
    return lax.dot_general(left, right, (((1,), (1,)), ((), ())), preferred_element_type=F32)


def dot_tn(left, right):
    return lax.dot_general(left, right, (((0,), (0,)), ((), ())), preferred_element_type=F32)


def wait_bytes(ref, sem):
    pltpu.make_async_copy(ref, ref, sem).wait()


def for_peers(me, experts, visit):
    if experts != 64:
        for step in range(1, experts):
            visit(lax.rem(me + step, experts))
        return
    my_z, my_y, my_core = me // 8, lax.rem(me // 2, 4), lax.rem(me, 2)
    near = [lax.rem(my_y + q // 2, 4) * 2 + lax.rem(my_core + q % 2, 2) for q in range(8)]

    def ring(step, carry):
        half = (step + 1) // 2
        base = lax.rem(my_z + 4 + half * (1 - 2 * lax.rem(step, 2)), 8) * 8
        for q in range(8):
            visit(base + near[q])
        return carry

    lax.fori_loop(0, 7, ring, 0)
    for q in range(1, 8):
        visit(my_z * 8 + near[q])


def column_of(wide):
    return wide[:, :1]


def kernel(
    experts, denominator,
    inputs, cotangent, lengths, gain, router, w_in_hbm, w_out_hbm, routes,
    grads_out, router_out, gain_out,
    w_in, w_out, hidden_of, grad_of, give, router_send, router_of, gain_send, gain_of,
    x_send, x_recv, y_send, y_relay, y_recv, g_send, g_recv, r_send, r_relay, r_recv,
    p_send, p_recv, f_send, f_recv, s_send, s_recv, t_send, t_recv,
    norm_send, norm_recv, diff_send, diff_recv, inner_send, inner_recv, norm_keep,
    mixed, joined, q_keep, row_scale, logit_keep, column, gain_part,
    plane_sem, weight_sem, h_sem, c_sem, give_sem, router_sem, gain_sem,
    x_sem, yr_sem, y_sem, g_sem, rr_sem, r_sem, p_sem, f_sem, s_sem, t_sem,
    norm_sem, diff_sem, inner_sem, o_sem,
    give_ss, router_ss, gain_ss, x_ss, yr_ss, y_ss, g_ss, rr_ss, r_ss, p_ss, f_ss, s_ss, t_ss,
    norm_ss, diff_ss, inner_ss, o_ss,
):
    x = lax.axis_index("section")
    me = lax.axis_index("expert")
    micros, tokens, width = inputs.shape
    sections = 4
    hidden = w_out.shape[1]
    slots = 2 * experts
    piece = width // sections
    owners = s_send.shape[0]
    stride = experts // owners
    ms = range(micros)

    def cols(q):
        return pl.ds(pl.multiple_of(q * piece, piece), piece)

    def send(source, target, send_sem, recv_sem, section, expert):
        pltpu.make_async_remote_copy(
            src_ref=source, dst_ref=target, send_sem=send_sem, recv_sem=recv_sem,
            device_id={"section": section, "expert": expert}, device_id_type=MESH,
        ).start()

    for m in ms:
        pltpu.make_async_copy(inputs.at[m, :, cols(x)], hidden_of.at[0, m], h_sem.at[m]).start()
    loads = []
    for q in range(sections):
        loads.append(pltpu.make_async_copy(w_in_hbm.at[0, 0, pl.ds(q * piece, piece)], w_in.at[q], weight_sem.at[0, q]))
    for q in range(sections):
        loads.append(pltpu.make_async_copy(w_out_hbm.at[0, 0, :, pl.ds(q * piece, piece)], w_out.at[q], weight_sem.at[1, q]))
    for load in loads:
        load.start()
    for m in ms:
        pltpu.make_async_copy(cotangent.at[m, :, cols(x)], grad_of.at[sections, m], c_sem.at[m]).start()

    barrier = pltpu.get_barrier_semaphore()

    def greet(peer):
        pl.semaphore_signal(barrier, inc=1, device_id={"section": x, "expert": peer}, device_id_type=MESH)

    for_peers(me, experts, greet)
    others = [lax.rem(x + step, sections) for step in (1, 3, 2)]
    for other in others:
        pl.semaphore_signal(barrier, inc=1, device_id={"section": other, "expert": me}, device_id_type=MESH)

    column[...] = jnp.zeros_like(column)
    gain_part[...] = jnp.zeros_like(gain_part)
    expert_codes = lax.broadcasted_iota(jnp.int32, (tokens, experts), 1)
    earlier = (
        lax.broadcasted_iota(jnp.int32, (tokens, tokens), 1)
        < lax.broadcasted_iota(jnp.int32, (tokens, tokens), 0)
    ).astype(F32).astype(BF16)
    slot_codes = lax.broadcasted_iota(jnp.int32, (tokens, slots), 1).astype(F32)
    positions = lax.broadcasted_iota(jnp.int32, (tokens, 1), 0)
    for m in ms:
        live = positions < lengths[m : m + 1, :]
        tables = []
        for k in range(2):
            choice = routes[0, m][:, k : k + 1]
            marked = (choice == expert_codes).astype(F32)
            rank = jnp.sum(marked * dot_nn(earlier, marked.astype(BF16)), axis=1, keepdims=True)
            slot = choice.astype(F32) * 2.0 + rank
            tables.append(((slot == slot_codes) & live).astype(F32))
        give[x, m] = jnp.concatenate(tables, axis=0).astype(BF16)
    eye = (
        lax.broadcasted_iota(jnp.int32, (experts, experts), 0)
        == lax.broadcasted_iota(jnp.int32, (experts, experts), 1)
    ).astype(F32).astype(BF16)
    for q in range(sections):
        router_send[q] = dot_nt(eye, router[0, q * piece : (q + 1) * piece, :]).astype(BF16)
        gain_send[q] = gain[:, q * piece : (q + 1) * piece]
    router_of[x] = router_send[x]
    gain_of[x] = gain_send[x]
    fold = (
        lax.broadcasted_iota(jnp.int32, (slots, experts), 0) // 2
        == lax.broadcasted_iota(jnp.int32, (slots, experts), 1)
    ).astype(F32).astype(BF16)

    pl.semaphore_wait(barrier, experts - 1 + sections - 1)
    for other in others:
        pl.semaphore_signal(plane_sem, inc=1, device_id={"section": other, "expert": me}, device_id_type=MESH)
    for other in others:
        send(gain_send.at[other], gain_of.at[x], gain_ss, gain_sem.at[x], other, me)
        send(give.at[x], give.at[x], give_ss, give_sem.at[x], other, me)
        send(router_send.at[other], router_of.at[x], router_ss, router_sem.at[x], other, me)
    pl.semaphore_wait(plane_sem, sections - 1)

    def share(values, sends, receives, send_sem, recv_sem, j, m):
        sends[j, m] = values
        for slot, other in enumerate(others):
            send(sends.at[j, m], receives.at[j, m, slot], send_sem.at[j, m], recv_sem.at[j, m], other, me)

    def shared(sends, receives, recv_sem, j, m):
        wait_bytes(receives.at[j, m], recv_sem.at[j, m])
        return sends[j, m] + receives[j, m, 0] + receives[j, m, 1] + receives[j, m, 2]

    def wide(values):
        return jnp.broadcast_to(values, (tokens, 128))

    def signs(j, m):
        return dot_nn(give[j, m, :tokens] - give[j, m, tokens:], fold)

    def scales(j, m):
        total = norm_keep[j, m]
        scale = lax.rsqrt(total[:, 0:1] / width + EPSILON)
        margin = total[:, 1:2] * scale
        return scale, jax.nn.sigmoid(margin), jax.nn.sigmoid(-margin)

    def dispatch(values, sends, receives, send_sem, recv_sem, j, m):
        sends[j, m] = dot_tn(give[j, m], values).astype(BF16).reshape(experts, 2, piece)
        target, arrive, leave = receives.at[m, x, me], recv_sem.at[m, x], send_sem.at[j, m]
        for_peers(me, experts, lambda peer: send(sends.at[j, m, peer], target, leave, arrive, j, peer))

        @pl.when(x == j)
        def _():
            pltpu.make_async_copy(sends.at[j, m, me], target, arrive).start()

        @pl.when(x != j)
        def _():
            send(sends.at[j, m, me], target, leave, arrive, j, me)

    def forward_send(j, m):
        values = hidden_of[j, m].astype(F32)
        rows = (values * gain_of[j]).astype(BF16)
        dispatch(jnp.concatenate([rows, rows], axis=0), x_send, x_recv, x_ss, x_sem, j, m)
        logits = dot_nt(rows, router_of[j])
        margin = jnp.sum(signs(j, m) * logits, axis=1, keepdims=True)
        square = jnp.sum(values * values, axis=1, keepdims=True)
        lanes = lax.broadcasted_iota(jnp.int32, (tokens, 128), 1)
        share(jnp.where(lanes == 0, square, jnp.where(lanes == 1, margin, 0.0)), norm_send, norm_recv, norm_ss, norm_sem, j, m)

    def settle(j, m):
        norm_keep[j, m] = shared(norm_send, norm_recv, norm_sem, j, m)

    def backward_send(j, m):
        _, first, second = scales(j, m)
        grad = grad_of[j + 1, m].astype(F32)
        pair = jnp.concatenate([(first * grad).astype(BF16), (second * grad).astype(BF16)], axis=0)
        dispatch(pair, g_send, g_recv, g_ss, g_sem, j, m)

    near_first = [lax.rem(x + step, sections) for step in (0, 1, 3, 2)]
    far_first = [lax.rem(x + step, sections) for step in (2, 1, 3)]

    def expert_forward(j, m):
        square = jnp.zeros((slots, 1), F32)
        for index, q in enumerate(near_first):
            wait_bytes(x_recv.at[m, q], x_sem.at[m, q])
            rows = x_recv[m, q].reshape(slots, piece)
            if m == 0:
                wait_bytes(w_in.at[q], weight_sem.at[0, q])
            part = dot_nn(rows, w_in[q])
            mixed[m] = part if index == 0 else mixed[m] + part
            plain = rows.astype(F32) / gain_send[q]
            square += jnp.sum(plain * plain, axis=1, keepdims=True)
        scale = lax.rsqrt(square / width + EPSILON)
        row_scale[m] = jnp.broadcast_to(scale, (slots, 128))
        gate, up = mixed[m, :, :hidden] * scale, mixed[m, :, hidden:] * scale
        mixed[m, :, :hidden] = gate
        mixed[m, :, hidden:] = up
        activated = (gate * jax.nn.sigmoid(gate) * up).astype(BF16)
        for q in far_first + [x]:
            if m == 0:
                wait_bytes(w_out.at[q], weight_sem.at[1, q])
            result = dot_nn(activated, w_out[q]).astype(BF16).reshape(experts, 2, piece)
            if q is x:
                y_relay[j, m] = result
            else:
                y_send[m, q] = result
                send(y_send.at[m, q], y_relay.at[j, m], yr_ss.at[m], yr_sem.at[j, m], q, me)

    def relay(buffer, target, bulk_sem, send_sem, recv_sem, j, m):
        @pl.when(x != j)
        def _():
            wait_bytes(buffer.at[j, m], bulk_sem.at[j, m])

        own = target.at[j, m, me]
        pltpu.make_async_copy(buffer.at[j, m, me], own, recv_sem.at[j, m]).start()
        for_peers(me, experts, lambda peer: send(buffer.at[j, m, peer], own, send_sem.at[j, m], recv_sem.at[j, m], x, peer))

    def choices(j, m):
        return dot_nn(give[j, m], y_recv[j, m].reshape(slots, piece))

    def forward_combine(j, m):
        wait_bytes(y_recv.at[j, m], y_sem.at[j, m])
        per_choice = choices(j, m)
        _, first, second = scales(j, m)
        combined = first * per_choice[:tokens] + second * per_choice[tokens:]
        hidden_of[j + 1, m] = (hidden_of[j, m].astype(F32) + combined).astype(BF16)

    def learn(j):
        @pl.when(x != j)
        def _():
            wait_bytes(gain_of.at[j], gain_sem.at[j])
            wait_bytes(give.at[j], give_sem.at[j])
            wait_bytes(router_of.at[j], router_sem.at[j])

    learn(0)
    for m in ms:
        wait_bytes(hidden_of.at[0, m], h_sem.at[m])
        forward_send(0, m)
    for m in ms:
        settle(0, m)

    def forward_stage(j, carry):
        for m in ms:
            @pl.when(x == j)
            def _():
                expert_forward(j, m)

            relay(y_relay, y_recv, yr_sem, y_ss, y_sem, j, m)

        @pl.when(j < sections - 1)
        def _():
            learn(j + 1)
            for m in ms:
                forward_combine(j, m)
                forward_send(j + 1, m)
            for m in ms:
                settle(j + 1, m)

        @pl.when(j == sections - 2)
        def _():
            for m in ms:
                wait_bytes(grad_of.at[sections, m], c_sem.at[m])
                backward_send(sections - 1, m)

        return carry

    lax.fori_loop(0, sections, forward_stage, 0)

    def expert_backward(j, m):
        for index, q in enumerate(near_first):
            wait_bytes(g_recv.at[m, q], g_sem.at[m, q])
            part = dot_nt(g_recv[m, q].reshape(slots, piece), w_out[q])
            act_grad = part if index == 0 else act_grad + part
        gate, up = mixed[m, :, :hidden], mixed[m, :, hidden:]
        sigmoid_gate = jax.nn.sigmoid(gate)
        joined[:, :hidden] = (act_grad * up * sigmoid_gate * (1.0 + gate * (1.0 - sigmoid_gate))).astype(BF16)
        joined[:, hidden:] = (act_grad * gate * sigmoid_gate).astype(BF16)
        for q in far_first + [x]:
            result = dot_nt(joined[...], w_in[q]).astype(BF16).reshape(experts, 2, piece)
            r_send[m, q] = result
            if q is x:
                r_relay[j, m] = result
            else:
                send(r_send.at[m, q], r_relay.at[j, m], rr_ss.at[m], rr_sem.at[j, m], q, me)

    def differ(j, m):
        @pl.when(j == sections - 1)
        def _():
            wait_bytes(y_recv.at[j, m], y_sem.at[j, m])

        per_choice = choices(j, m)
        grad = grad_of[j + 1, m].astype(F32)
        difference = jnp.sum(grad * (per_choice[:tokens] - per_choice[tokens:]), axis=1, keepdims=True)
        share(wide(difference), diff_send, diff_recv, diff_ss, diff_sem, j, m)

    def pick_choice(j, m):
        difference = column_of(shared(diff_send, diff_recv, diff_sem, j, m))
        _, first, second = scales(j, m)
        pick = first * second * difference
        logit_keep[m] = (pick * signs(j, m)).astype(BF16)

        @pl.when(x == j)
        def _():
            lanes = lax.broadcasted_iota(jnp.int32, (2 * tokens, 128), 1)
            picks = jnp.where(lanes == 0, jnp.concatenate([pick, -pick], axis=0), 0.0).astype(BF16)
            p_send[m] = dot_tn(give[j, m], picks).astype(BF16).reshape(experts, 2, 128)
            own = p_recv.at[m, me]
            pltpu.make_async_copy(p_send.at[m, me], own, p_sem.at[m]).start()
            for_peers(me, experts, lambda peer: send(p_send.at[m, peer], own, p_ss.at[m], p_sem.at[m], x, peer))

    def parameter_sums():
        for m in ms:
            wait_bytes(p_recv.at[m], p_sem.at[m])
            scale = column_of(row_scale[m])
            weight = p_recv[m].reshape(slots, 128)[:, :1].astype(F32) * scale
            for q in range(sections):
                rows = x_recv[m, q].reshape(slots, piece).astype(F32)
                row_grads = r_send[m, q].reshape(slots, piece).astype(F32)
                column[q] += jnp.sum(rows * weight, axis=0, keepdims=True)
                gain_part[q] += jnp.sum(row_grads * (rows * scale), axis=0, keepdims=True)
        mine = (lax.broadcasted_iota(jnp.int32, (8, experts), 1) == me).astype(F32).astype(BF16)
        for q in range(sections):
            own_router = dot_nn(mine, router_send[q])[:1]
            total = (gain_part[q] + own_router * column[q]) / gain_send[q]
            for b in range(owners // sections):
                s_send[q * (owners // sections) + b] = total[:, b * 128 : (b + 1) * 128]
        f_send[0] = jnp.concatenate(
            [jnp.concatenate([column[0], column[1]], axis=1), jnp.concatenate([column[2], column[3]], axis=1)], axis=0
        ).astype(BF16)
        for b in range(owners):
            @pl.when(me == b * stride)
            def _():
                pltpu.make_async_copy(s_send.at[b], s_recv.at[me], s_sem).start()

            @pl.when(me != b * stride)
            def _():
                send(s_send.at[b], s_recv.at[me], s_ss, s_sem, x, b * stride)

        pltpu.make_async_copy(f_send.at[0], f_recv.at[me], f_sem).start()
        for_peers(me, experts, lambda peer: send(f_send.at[0], f_recv.at[me], f_ss, f_sem, x, peer))

    def owner_sum():
        wait_bytes(s_recv, s_sem)
        t_send[0] = jnp.sum(s_recv[:, 0, :], axis=0, keepdims=True) / denominator
        own = t_recv.at[me // stride]
        pltpu.make_async_copy(t_send.at[0], own, t_sem).start()
        for_peers(me, experts, lambda peer: send(t_send.at[0], own, t_ss, t_sem, x, peer))

    def backward_gather(j, m):
        wait_bytes(r_recv.at[j, m], r_sem.at[j, m])
        both = give[j, m, :tokens] + give[j, m, tokens:]
        scaled = (
            dot_nn(both, r_recv[j, m].reshape(slots, piece)) + dot_nn(logit_keep[m], router_of[j])
        ) * gain_of[j]
        q_keep[m] = scaled
        scale, _, _ = scales(j, m)
        inner = jnp.sum(scaled * (hidden_of[j, m].astype(F32) * scale), axis=1, keepdims=True)
        share(wide(inner), inner_send, inner_recv, inner_ss, inner_sem, j, m)

    def backward_finish(j, m):
        scale, _, _ = scales(j, m)
        inner = column_of(shared(inner_send, inner_recv, inner_sem, j, m)) / width
        centred = hidden_of[j, m].astype(F32) * scale
        grad = grad_of[j + 1, m].astype(F32)
        grad_of[j, m] = (grad + scale * (q_keep[m] - centred * inner)).astype(BF16)

        @pl.when(j > 0)
        def _():
            backward_send(j - 1, m)

        target = grads_out.at[0, m, :, cols(x)]

        @pl.when(x == j)
        def _():
            pltpu.make_async_copy(grad_of.at[j, m], target, o_sem.at[m]).start()

        @pl.when(x != j)
        def _():
            send(grad_of.at[j, m], target, o_ss.at[j, m], o_sem.at[m], j, me)

    def backward_stage(step, carry):
        j = sections - 1 - step
        for m in ms:
            @pl.when(x == j)
            def _():
                expert_backward(j, m)

            relay(r_relay, r_recv, rr_sem, r_ss, r_sem, j, m)
        for m in ms:
            differ(j, m)
        for m in ms:
            pick_choice(j, m)

        @pl.when(x == j)
        def _():
            parameter_sums()

        for m in ms:
            backward_gather(j, m)

        @pl.when((x == j) & (lax.rem(me, stride) == 0))
        def _():
            owner_sum()

        for m in ms:
            backward_finish(j, m)
        return carry

    lax.fori_loop(0, sections, backward_stage, 0)

    wait_bytes(f_recv, f_sem)
    half = width // 2
    router_out[:, :half] = f_recv[:, 0, :].astype(F32) / denominator
    router_out[:, half:] = f_recv[:, 1, :].astype(F32) / denominator
    wait_bytes(t_recv, t_sem)
    for b in range(owners):
        gain_out[:, b * 128 : (b + 1) * 128] = t_recv[b]

    rest = pl.ds(0, experts - 1)
    for m in ms:
        wait_bytes(grad_of.at[pl.ds(0, sections), m], o_sem.at[m])
        wait_bytes(y_send.at[m, pl.ds(0, 3)], yr_ss.at[m])
        wait_bytes(r_send.at[m, pl.ds(0, 3)], rr_ss.at[m])
        wait_bytes(p_send.at[m, rest], p_ss.at[m])
    wait_bytes(gain_send.at[pl.ds(0, 3)], gain_ss)
    wait_bytes(give.at[pl.ds(0, 3)], give_ss)
    wait_bytes(router_send.at[pl.ds(0, 3)], router_ss)
    wait_bytes(f_recv.at[rest], f_ss)

    @pl.when(lax.rem(me, stride) == 0)
    def _():
        wait_bytes(s_send.at[pl.ds(0, owners - 1)], s_ss)
        wait_bytes(s_recv.at[rest], t_ss)

    @pl.when(lax.rem(me, stride) != 0)
    def _():
        wait_bytes(s_send, s_ss)

    def drain(j, carry):
        for m in ms:
            for buffer, sem in ((x_send, x_ss), (g_send, g_ss), (y_relay, y_ss), (r_relay, r_ss)):
                wait_bytes(buffer.at[j, m, rest], sem.at[j, m])
            for buffer, sem in ((norm_recv, norm_ss), (diff_recv, diff_ss), (inner_recv, inner_ss)):
                wait_bytes(buffer.at[j, m], sem.at[j, m])

            @pl.when(x != j)
            def _():
                wait_bytes(x_send.at[j, m, 0], x_ss.at[j, m])
                wait_bytes(g_send.at[j, m, 0], g_ss.at[j, m])
                wait_bytes(grad_of.at[j, m], o_ss.at[j, m])

        return carry

    lax.fori_loop(0, sections, drain, 0)


def solution(mesh):
    sections, experts = mesh.shape["section"], mesh.shape["expert"]

    def local(inputs, cotangent, lengths, norm_gain, router, expert_in, expert_out, routes):
        micros, tokens, width = inputs.shape
        hidden = expert_out.shape[2]
        piece = width // sections
        owners = width // 128
        slots = 2 * experts
        vmem = pl.BlockSpec(memory_space=pltpu.VMEM)
        hbm = pl.BlockSpec(memory_space=pl.ANY)
        DMA = pltpu.SemaphoreType.DMA
        steps = pltpu.VMEM((sections, micros, experts, 2, piece), BF16)
        parts = pltpu.VMEM((micros, sections, experts, 2, piece), BF16)
        small = pltpu.VMEM((micros, experts, 2, 128), BF16)
        stat = pltpu.VMEM((sections, micros, tokens, 128), F32)
        stats = pltpu.VMEM((sections, micros, sections - 1, tokens, 128), F32)
        rows = pltpu.VMEM((sections, 1, piece), F32)
        routing = pltpu.VMEM((sections, experts, piece), BF16)
        each, parted, single = DMA((sections, micros)), DMA((micros, sections)), DMA((micros,))
        grads, router_rows, gain_row = pl.pallas_call(
            functools.partial(kernel, experts, float(micros * 2 * tokens)),
            out_shape=(
                jax.ShapeDtypeStruct((1, micros, tokens, width), BF16),
                jax.ShapeDtypeStruct((experts, width), F32),
                jax.ShapeDtypeStruct((1, width), F32),
            ),
            in_specs=[hbm, hbm, vmem, vmem, vmem, hbm, hbm, vmem],
            out_specs=(hbm, vmem, vmem),
            scratch_shapes=[
                pltpu.VMEM((sections, piece, 2 * hidden), BF16),
                pltpu.VMEM((sections, hidden, piece), BF16),
                pltpu.VMEM((sections, micros, tokens, piece), BF16),
                pltpu.VMEM((sections + 1, micros, tokens, piece), BF16),
                pltpu.VMEM((sections, micros, 2 * tokens, slots), BF16),
                routing, routing, rows, rows,
                steps, parts, parts, steps, steps, steps, parts, parts, steps, steps,
                small, small,
                pltpu.VMEM((1, 2, width // 2), BF16),
                pltpu.VMEM((experts, 2, width // 2), BF16),
                pltpu.VMEM((owners, 1, 128), F32),
                pltpu.VMEM((experts, 1, 128), F32),
                pltpu.VMEM((1, 1, 128), F32),
                pltpu.VMEM((owners, 1, 128), F32),
                stat, stats, stat, stats, stat, stats, stat,
                pltpu.VMEM((micros, slots, 2 * hidden), F32),
                pltpu.VMEM((slots, 2 * hidden), BF16),
                pltpu.VMEM((micros, tokens, piece), F32),
                pltpu.VMEM((micros, slots, 128), F32),
                pltpu.VMEM((micros, tokens, experts), BF16),
                rows, rows,
                pltpu.SemaphoreType.REGULAR, DMA((2, sections)), single, single,
                DMA((sections,)), DMA((sections,)), DMA((sections,)),
                parted, each, each, parted, each, each, single, DMA, DMA, DMA,
                each, each, each, single,
                DMA, DMA, DMA, each, single, each, each, single, each, single, DMA, DMA, DMA,
                each, each, each, each,
            ],
            compiler_params=pltpu.CompilerParams(
                collective_id=0, has_side_effects=True, vmem_limit_bytes=60 * 1024 * 1024
            ),
        )(inputs, cotangent, lengths, norm_gain, router, expert_in, expert_out, routes)
        return grads, router_rows.T[None], gain_row

    in_specs = (
        P(None, "expert", None),
        P(None, "expert", None),
        P(None, "expert"),
        P("section", None),
        P("section", None, None),
        P("section", "expert", None, None),
        P("section", "expert", None, None),
        P("section", None, "expert", None),
    )
    out_specs = (P("section", None, "expert", None), P("section", None, None), P("section", None))
    return jax.shard_map(local, mesh=mesh, in_specs=in_specs, out_specs=out_specs, check_vma=False)
```

time: 406 us -> 334 us (0.82)
  Pallas kernels: 395 us -> 323 us
    pallas_call x1, Pallas kernels: 395 us -> 323 us  [local(): pl.pallas_call(functools.partial(kernel, experts, float(micros * 2 * toke...]
where the time goes in v3:
time: 334 us
  Pallas kernels  323 us (97%)
  local copies, waits for them, and re-layouts  9.71 us (3%)
    pallas_call x1, Pallas kernels, local(): pl.pallas_call(functools.partial(kernel, experts, float(micros * 2 * toke...  323 us
    unnamed x6, local copies, waits for them, and re-layouts  9.71 us

profile of v3, /device:TPU:1, one launch (start us, length us, event | category | flops | bytes accessed | tf_op | source)
XLA Modules:
  0.0 333.8 jit_solution(4237777175273644848)
XLA Ops:
  0.6 1.3 copy.11.lengths
  1.9 1.4 copy.13.routes
  3.3 2.0 copy.12.router
  5.3 323.4 %shard_map.103 = (bf16[1,2,64,2048]{3,2,1,0:T(8,128)(2,1)}, f32[64,2048]{1,0:T(8,128)}, f32[1,2048]{1,0:T(1,128)}) custom-call(bf16[2,64,2048]{2,1,0:T(8,128)(2,1)} %inputs.1, bf16[2,64,2048]{2,1,0:T(8,128)(2,1)} %cotangent.1, s32[2,1]{1,0:T(2,128)} %copy.11.lengths, f32[1,2048]{1,0:T(1,128)} %gain.1, bf16[1,2048,64]{2,1,0:T(8,128)(2,1)} %copy.12.router, ...), custom_call_target="tpu_custom_call" | custom-call | tf_op jit(solution)/shard_map/pallas_call | solution.py:506
  328.7 1.9 copy.17
  330.6 1.9 copy.18
  332.5 1.3 copy.19

commit v4 on v3

--- a/solution.py
+++ b/solution.py
@@ -49,6 +49,26 @@
         visit(my_z * 8 + near[q])
 
 
+def for_half(me, experts, half, visit, own):
+    if experts != 64:
+        for peer in range(half * experts // 2, (half + 1) * experts // 2):
+            pl.when(peer != me)(functools.partial(visit, peer))
+            pl.when(peer == me)(own)
+        return
+    my_z, my_y, my_core = me // 8, lax.rem(me // 2, 4), lax.rem(me, 2)
+    near = [lax.rem(my_y + q // 2, 4) * 2 + lax.rem(my_core + q % 2, 2) for q in range(8)]
+
+    def ring(step, carry):
+        z = half * 4 + lax.rem(my_z + 2 + step, 4)
+        for q in range(1, 8):
+            visit(z * 8 + near[q])
+        pl.when(z != my_z)(lambda: visit(z * 8 + near[0]))
+        pl.when(z == my_z)(own)
+        return carry
+
+    lax.fori_loop(0, 4, ring, 0)
+
+
 def column_of(wide):
     return wide[:, :1]
 
@@ -57,7 +77,7 @@
     experts, denominator,
     inputs, cotangent, lengths, gain, router, w_in_hbm, w_out_hbm, routes,
     grads_out, router_out, gain_out,
-    w_in, w_out, hidden_of, grad_of, give, router_send, router_of, gain_send, gain_of,
+    w_in, w_out, hidden_of, grad_of, give, router_send, router_of, gain_send, gain_of, gain_inverse,
     x_send, x_recv, y_send, y_relay, y_recv, g_send, g_recv, r_send, r_relay, r_recv,
     p_send, p_recv, f_send, f_recv, s_send, s_recv, t_send, t_recv,
     norm_send, norm_recv, diff_send, diff_recv, inner_send, inner_recv, norm_keep,
@@ -136,6 +156,7 @@
     for q in range(sections):
         router_send[q] = dot_nt(eye, router[0, q * piece : (q + 1) * piece, :]).astype(BF16)
         gain_send[q] = gain[:, q * piece : (q + 1) * piece]
+        gain_inverse[q] = 1.0 / gain_send[q]
     router_of[x] = router_send[x]
     gain_of[x] = gain_send[x]
     fold = (
@@ -146,20 +167,26 @@
     pl.semaphore_wait(barrier, experts - 1 + sections - 1)
     for other in others:
         pl.semaphore_signal(plane_sem, inc=1, device_id={"section": other, "expert": me}, device_id_type=MESH)
-    for other in others:
-        send(gain_send.at[other], gain_of.at[x], gain_ss, gain_sem.at[x], other, me)
-        send(give.at[x], give.at[x], give_ss, give_sem.at[x], other, me)
-        send(router_send.at[other], router_of.at[x], router_ss, router_sem.at[x], other, me)
+
+    def publish():
+        for other in others:
+            send(gain_send.at[other], gain_of.at[x], gain_ss, gain_sem.at[x], other, me)
+            send(give.at[x], give.at[x], give_ss, give_sem.at[x], other, me)
+        for other in others:
+            send(router_send.at[other], router_of.at[x], router_ss, router_sem.at[x], other, me)
+
+    pl.when(x == 0)(publish)
     pl.semaphore_wait(plane_sem, sections - 1)
 
     def share(values, sends, receives, send_sem, recv_sem, j, m):
-        sends[j, m] = values
+        sends[j, m] = jnp.concatenate([values] * (128 // tokens), axis=0).T[:8]
         for slot, other in enumerate(others):
             send(sends.at[j, m], receives.at[j, m, slot], send_sem.at[j, m], recv_sem.at[j, m], other, me)
 
     def shared(sends, receives, recv_sem, j, m):
         wait_bytes(receives.at[j, m], recv_sem.at[j, m])
-        return sends[j, m] + receives[j, m, 0] + receives[j, m, 1] + receives[j, m, 2]
+        total = sends[j, m] + receives[j, m, 0] + receives[j, m, 1] + receives[j, m, 2]
+        return jnp.concatenate([total] * 16, axis=0).T[:tokens]
 
     def wide(values):
         return jnp.broadcast_to(values, (tokens, 128))
@@ -190,6 +217,11 @@
         values = hidden_of[j, m].astype(F32)
         rows = (values * gain_of[j]).astype(BF16)
         dispatch(jnp.concatenate([rows, rows], axis=0), x_send, x_recv, x_ss, x_sem, j, m)
+        if m == 0:
+            @pl.when(x != j)
+            def _():
+                wait_bytes(router_of.at[j], router_sem.at[j])
+
         logits = dot_nt(rows, router_of[j])
         margin = jnp.sum(signs(j, m) * logits, axis=1, keepdims=True)
         square = jnp.sum(values * values, axis=1, keepdims=True)
@@ -204,6 +236,11 @@
         grad = grad_of[j + 1, m].astype(F32)
         pair = jnp.concatenate([(first * grad).astype(BF16), (second * grad).astype(BF16)], axis=0)
         dispatch(pair, g_send, g_recv, g_ss, g_sem, j, m)
+
+    def bulk(sends, receives, send_sem, recv_sem, j, m, q):
+        for half in range(2):
+            part = pl.ds(half * experts // 2, experts // 2)
+            send(sends.at[m, q, part], receives.at[j, m, part], send_sem.at[m], recv_sem.at[j, m, half], q, me)
 
     near_first = [lax.rem(x + step, sections) for step in (0, 1, 3, 2)]
     far_first = [lax.rem(x + step, sections) for step in (2, 1, 3)]
@@ -217,7 +254,7 @@
                 wait_bytes(w_in.at[q], weight_sem.at[0, q])
             part = dot_nn(rows, w_in[q])
             mixed[m] = part if index == 0 else mixed[m] + part
-            plain = rows.astype(F32) / gain_send[q]
+            plain = rows.astype(F32) * gain_inverse[q]
             square += jnp.sum(plain * plain, axis=1, keepdims=True)
         scale = lax.rsqrt(square / width + EPSILON)
         row_scale[m] = jnp.broadcast_to(scale, (slots, 128))
@@ -233,16 +270,20 @@
                 y_relay[j, m] = result
             else:
                 y_send[m, q] = result
-                send(y_send.at[m, q], y_relay.at[j, m], yr_ss.at[m], yr_sem.at[j, m], q, me)
+                bulk(y_send, y_relay, yr_ss, yr_sem, j, m, q)
 
     def relay(buffer, target, bulk_sem, send_sem, recv_sem, j, m):
-        @pl.when(x != j)
-        def _():
-            wait_bytes(buffer.at[j, m], bulk_sem.at[j, m])
-
         own = target.at[j, m, me]
-        pltpu.make_async_copy(buffer.at[j, m, me], own, recv_sem.at[j, m]).start()
-        for_peers(me, experts, lambda peer: send(buffer.at[j, m, peer], own, send_sem.at[j, m], recv_sem.at[j, m], x, peer))
+        for half in range(2):
+            @pl.when(x != j)
+            def _():
+                wait_bytes(buffer.at[j, m, pl.ds(half * experts // 2, experts // 2)], bulk_sem.at[j, m, half])
+
+            for_half(
+                me, experts, half,
+                lambda peer: send(buffer.at[j, m, peer], own, send_sem.at[j, m], recv_sem.at[j, m], x, peer),
+                lambda: pltpu.make_async_copy(buffer.at[j, m, me], own, recv_sem.at[j, m]).start(),
+            )
 
     def choices(j, m):
         return dot_nn(give[j, m], y_recv[j, m].reshape(slots, piece))
@@ -259,12 +300,12 @@
         def _():
             wait_bytes(gain_of.at[j], gain_sem.at[j])
             wait_bytes(give.at[j], give_sem.at[j])
-            wait_bytes(router_of.at[j], router_sem.at[j])
 
     learn(0)
     for m in ms:
         wait_bytes(hidden_of.at[0, m], h_sem.at[m])
         forward_send(0, m)
+    pl.when(x != 0)(publish)
     for m in ms:
         settle(0, m)
 
@@ -310,7 +351,7 @@
             if q is x:
                 r_relay[j, m] = result
             else:
-                send(r_send.at[m, q], r_relay.at[j, m], rr_ss.at[m], rr_sem.at[j, m], q, me)
+                bulk(r_send, r_relay, rr_ss, rr_sem, j, m, q)
 
     def differ(j, m):
         @pl.when(j == sections - 1)
@@ -407,6 +448,12 @@
         def _():
             send(grad_of.at[j, m], target, o_ss.at[j, m], o_sem.at[m], j, me)
 
+    def pick_all(j):
+        for m in ms:
+            differ(j, m)
+        for m in ms:
+            pick_choice(j, m)
+
     def backward_stage(step, carry):
         j = sections - 1 - step
         for m in ms:
@@ -415,24 +462,31 @@
                 expert_backward(j, m)
 
             relay(r_relay, r_recv, rr_sem, r_ss, r_sem, j, m)
-        for m in ms:
-            differ(j, m)
-        for m in ms:
-            pick_choice(j, m)
-
-        @pl.when(x == j)
+
+        @pl.when(j == sections - 1)
+        def _():
+            pick_all(j)
+
+        @pl.when((j == 0) & (x == 0))
         def _():
             parameter_sums()
 
         for m in ms:
             backward_gather(j, m)
-
-        @pl.when((x == j) & (lax.rem(me, stride) == 0))
-        def _():
-            owner_sum()
-
-        for m in ms:
             backward_finish(j, m)
+            if m == 0:
+                @pl.when((j == 0) & (lax.rem(me, stride) == 0))
+                def _():
+                    owner_sum()
+
+        @pl.when(j > 0)
+        def _():
+            pick_all(j - 1)
+
+            @pl.when(x == j)
+            def _():
+                parameter_sums()
+
         return carry
 
     lax.fori_loop(0, sections, backward_stage, 0)
@@ -498,10 +552,12 @@
         steps = pltpu.VMEM((sections, micros, experts, 2, piece), BF16)
         parts = pltpu.VMEM((micros, sections, experts, 2, piece), BF16)
         small = pltpu.VMEM((micros, experts, 2, 128), BF16)
-        stat = pltpu.VMEM((sections, micros, tokens, 128), F32)
-        stats = pltpu.VMEM((sections, micros, sections - 1, tokens, 128), F32)
+        stat = pltpu.VMEM((sections, micros, 8, 128), F32)
+        stats = pltpu.VMEM((sections, micros, sections - 1, 8, 128), F32)
+        kept = pltpu.VMEM((sections, micros, tokens, 128), F32)
         rows = pltpu.VMEM((sections, 1, piece), F32)
         routing = pltpu.VMEM((sections, experts, piece), BF16)
+        halved = DMA((sections, micros, 2))
         each, parted, single = DMA((sections, micros)), DMA((micros, sections)), DMA((micros,))
         grads, router_rows, gain_row = pl.pallas_call(
             functools.partial(kernel, experts, float(micros * 2 * tokens)),
@@ -518,7 +574,7 @@
                 pltpu.VMEM((sections, micros, tokens, piece), BF16),
                 pltpu.VMEM((sections + 1, micros, tokens, piece), BF16),
                 pltpu.VMEM((sections, micros, 2 * tokens, slots), BF16),
-                routing, routing, rows, rows,
+                routing, routing, rows, rows, rows,
                 steps, parts, parts, steps, steps, steps, parts, parts, steps, steps,
                 small, small,
                 pltpu.VMEM((1, 2, width // 2), BF16),
@@ -527,7 +583,7 @@
                 pltpu.VMEM((experts, 1, 128), F32),
                 pltpu.VMEM((1, 1, 128), F32),
                 pltpu.VMEM((owners, 1, 128), F32),
-                stat, stats, stat, stats, stat, stats, stat,
+                stat, stats, stat, stats, stat, stats, kept,
                 pltpu.VMEM((micros, slots, 2 * hidden), F32),
                 pltpu.VMEM((slots, 2 * hidden), BF16),
                 pltpu.VMEM((micros, tokens, piece), F32),
@@ -536,7 +592,7 @@
                 rows, rows,
                 pltpu.SemaphoreType.REGULAR, DMA((2, sections)), single, single,
                 DMA((sections,)), DMA((sections,)), DMA((sections,)),
-                parted, each, each, parted, each, each, single, DMA, DMA, DMA,
+                parted, halved, each, parted, halved, each, single, DMA, DMA, DMA,
                 each, each, each, single,
                 DMA, DMA, DMA, each, single, each, each, single, each, single, DMA, DMA, DMA,
                 each, each, each, each,

time: 334 us -> 285 us (0.85)
  Pallas kernels: 323 us -> 275 us
    pallas_call x1, Pallas kernels: 323 us -> 275 us  [local(): pl.pallas_call(functools.partial(kernel, experts, float(micros * 2 * toke...]
where the time goes in v4:
time: 285 us
  Pallas kernels  275 us (96%)
  local copies, waits for them, and re-layouts  9.71 us (3%)
    pallas_call x1, Pallas kernels, local(): pl.pallas_call(functools.partial(kernel, experts, float(micros * 2 * toke...  275 us
    unnamed x6, local copies, waits for them, and re-layouts  9.71 us

profile of v4, /device:TPU:1, one launch (start us, length us, event | category | flops | bytes accessed | tf_op | source)
XLA Modules:
  0.0 285.0 jit_solution(6021170392199014671)
XLA Ops:
  0.6 1.3 copy.11.lengths
  1.9 1.4 copy.13.routes
  3.3 2.0 copy.12.router
  5.3 274.7 %shard_map.103 = (bf16[1,2,64,2048]{3,2,1,0:T(8,128)(2,1)}, f32[64,2048]{1,0:T(8,128)}, f32[1,2048]{1,0:T(1,128)}) custom-call(bf16[2,64,2048]{2,1,0:T(8,128)(2,1)} %inputs.1, bf16[2,64,2048]{2,1,0:T(8,128)(2,1)} %cotangent.1, s32[2,1]{1,0:T(2,128)} %copy.11.lengths, f32[1,2048]{1,0:T(1,128)} %gain.1, bf16[1,2048,64]{2,1,0:T(8,128)(2,1)} %copy.12.router, ...), custom_call_target="tpu_custom_call" | custom-call | tf_op jit(solution)/shard_map/pallas_call | solution.py:562
  280.0 1.9 copy.17
  281.9 1.9 copy.18
  283.7 1.3 copy.19
